TPU v7x, 256 devices: a whole 4x4x8 slice. The times are simulated.
256 devices in a mesh: seq: 32 (over y_hi, z, core), head: 8 (over x, y_lo).
Axes of the slice: x: 4, y: 4 (y_hi: 2, y_lo: 2; y = y_hi * 2 + y_lo), z: 8, core: 2. Of those that a mesh axis runs over, the one named last changes fastest.
Arguments:
- queries: bfloat16 [49152, 4096], P('seq', 'head'), may hold values from -6 to 6, as said below
- keys: bfloat16 [49152, 2048], P('seq', 'head'), may hold values from -6 to 6
- values: bfloat16 [49152, 2048], P('seq', 'head'), may hold values from -6 to 6
- q_gain: float32 [128], replicated, may hold values from -0.5 to 5
- k_gain: float32 [128], replicated, may hold values from -0.5 to 5
- positions: int32 [49152], P('seq'), may hold values from 2048 to 52222, as said below
- prefix_cache: bfloat16 [32, 2048, 4096], P('seq', 'head'), may hold values from -6 to 6
- owner: int32 [1], replicated, may hold values from 0 to 31
Outputs:
- attended: bfloat16 [49152, 4096], P('seq', 'head')
Inputs may be any that keep to these rules, and one draw needn't show every extreme that they name: queries and keys are of order one. positions[i] = positions[0] + i, and positions[0] is 2048 or more and under 2048 + 1024.
All inputs are finite; a program needn't handle non-finite values.
Results may differ from a plain program's by a relative error of at most 0.02.
Values may be sent and summed in bfloat16 or wider, within the bound.
No kernel may reach another device: no remote copies, remote signals or barrier semaphores. Data moves between devices by JAX's collectives and lax.ppermute only.
A program may use at most 128 MiB of HBM per device.

v0:
```python
import jax
import jax.numpy as jnp
from jax import lax
from jax.sharding import PartitionSpec as P

WINDOW = 1024
QSCALAR = 168
BLOCK = 512


def passed_along(block, axis, distance):
    devices = range(lax.axis_size(axis))
    route = [(i - distance, i) for i in devices if i - distance in devices]
    return lax.ppermute(block, axis, route)


def spread(array, axis, root):
    mine = lax.axis_index(axis) == root
    return lax.psum(jnp.where(mine, array, jnp.zeros_like(array)), axis)


def norm_rope(rows_in, gain, pos, factor):
    mean_sq = jnp.mean(rows_in * rows_in, axis=-1, keepdims=True)
    normed = rows_in / jnp.sqrt(mean_sq + 1e-06) * (1.0 + gain)
    half = rows_in.shape[-1] // 2
    freq = 10000.0 ** (-(jnp.arange(half).astype(jnp.float32) * 2.0) / rows_in.shape[-1])
    angle = pos.astype(jnp.float32)[:, None] * freq[None, :]
    cosine = jnp.cos(angle)[:, None, :]
    sine = jnp.sin(angle)[:, None, :]
    first = normed[..., :half]
    second = normed[..., half:]
    return (
        jnp.concatenate([first * cosine - second * sine, second * cosine + first * sine], axis=-1)
        * factor
    )


def on_device(queries, keys, values, q_gain, k_gain, positions, prefix_cache, owner):
    local_rows = queries.shape[0]
    head_size = q_gain.shape[0]
    local_q = queries.shape[1] // head_size
    local_kv = keys.shape[1] // head_size
    group = local_q // local_kv
    query = norm_rope(
        queries.astype(jnp.float32).reshape(local_rows, local_q, head_size),
        q_gain,
        positions,
        QSCALAR ** (-0.5),
    ).astype(jnp.bfloat16)
    key = norm_rope(
        keys.astype(jnp.float32).reshape(local_rows, local_kv, head_size), k_gain, positions, 1.0
    ).astype(jnp.bfloat16)
    stacked = jnp.stack([key.reshape(local_rows, local_kv * head_size), values], axis=0)
    whole_prev = passed_along(stacked, "seq", 1)
    earlier = whole_prev[:, local_rows - WINDOW :]
    extended = jnp.concatenate([earlier, stacked], axis=1).reshape(
        2, WINDOW + local_rows, local_kv, head_size
    )
    root = owner[0]
    slab = spread(prefix_cache, "seq", root)
    mine = lax.all_to_all(slab, "head", split_axis=2, concat_axis=1, tiled=True)
    mine = mine.reshape(mine.shape[1], local_kv, 2, head_size)
    prefix_key = mine[:, :, 0, :]
    prefix_value = mine[:, :, 1, :]
    offset = lax.axis_index("seq") * local_rows

    def one_block(index):
        start = index * BLOCK
        query_block = lax.dynamic_slice_in_dim(query, start, BLOCK, 0).reshape(
            BLOCK, local_kv, group, head_size
        )
        key_block = lax.dynamic_slice_in_dim(extended[0], start, WINDOW + BLOCK, 0)
        value_block = lax.dynamic_slice_in_dim(extended[1], start, WINDOW + BLOCK, 0)
        band = jnp.einsum(
            "ikgd,jkd->kgij", query_block, key_block, preferred_element_type=jnp.float32
        )
        row_pos = offset + start + jnp.arange(BLOCK, dtype=jnp.int32)
        col_pos = offset + start + jnp.arange(WINDOW + BLOCK, dtype=jnp.int32) - WINDOW
        valid = (
            (col_pos[None, :] >= 0)
            & (col_pos[None, :] <= row_pos[:, None])
            & (col_pos[None, :] > row_pos[:, None] - WINDOW)
        )
        band = jnp.where(valid[None, None], band, -jnp.inf)
        pre = jnp.einsum(
            "ikgd,tkd->kgit", query_block, prefix_key, preferred_element_type=jnp.float32
        )
        top = jnp.maximum(jnp.max(band, axis=-1), jnp.max(pre, axis=-1))
        exp_band = jnp.exp(band - top[..., None])
        exp_pre = jnp.exp(pre - top[..., None])
        total = jnp.sum(exp_band, axis=-1) + jnp.sum(exp_pre, axis=-1)
        summed = jnp.einsum(
            "kgij,jkd->kgid",
            exp_band.astype(jnp.bfloat16),
            value_block,
            preferred_element_type=jnp.float32,
        )
        summed = summed + jnp.einsum(
            "kgit,tkd->kgid",
            exp_pre.astype(jnp.bfloat16),
            prefix_value,
            preferred_element_type=jnp.float32,
        )
        result = summed / total[..., None]
        return (
            jnp.transpose(result, (2, 0, 1, 3))
            .reshape(BLOCK, local_q * head_size)
            .astype(jnp.bfloat16)
        )

    blocks = lax.map(one_block, jnp.arange(local_rows // BLOCK, dtype=jnp.int32))
    return blocks.reshape(local_rows, local_q * head_size)


def solution(mesh):
    return jax.shard_map(
        on_device,
        mesh=mesh,
        in_specs=(
            P("seq", "head"),
            P("seq", "head"),
            P("seq", "head"),
            P(),
            P(),
            P("seq"),
            P("seq", "head", None),
            P(),
        ),
        out_specs=P("seq", "head"),
        check_vma=False,
    )
```

profile of v0, /device:TPU:1, one launch (start us, length us, event | category | flops | bytes accessed | tf_op | source)
XLA Modules:
  0.0 521.0 jit_solution(8739083198048859885)
XLA Ops:
  7.2 10.1 %copy.57 = bf16[1,256,4096]{1,0,2:T(2,128)(2,1)} copy(bf16[1,256,4096]{2,1,0:T(8,128)(2,1)} %param.16) | data formatting | bytes 4194304 | tf_op args[6]
  17.2 6.1 %broadcast_select_fusion = bf16[1,256,4096]{1,0,2:T(2,128)(2,1)} fusion(bf16[1,256,4096]{1,0,2:T(2,128)(2,1)} %copy.57, pred[]{:T(512)S(6)} %eq.3), kind=kLoop, calls=%fused_computation.39 | loop fusion | flops 1048576 | bytes 4194305 | tf_op jit(solution)/shard_map/jit(_where)/select_n | solution.py:19
  42.3 5.2 %collective-permute-start = (bf16[2,1536,256]{1,2,0:T(8,128)(2,1)}, bf16[2,1536,256]{1,2,0:T(8,128)(2,1)}, u32[]{:S(2)}, u32[]{:S(2)}) collective-permute-start(bf16[2,1536,256]{1,2,0:T(8,128)(2,1)} %pad_maximum_fusion), channel_id=1, source_target_pairs={{0,8},{8,16},{16,24},{24,32},{32,40},{40,48},{48,56},{56,64},{64,7... | collective-permute-start | bytes 4718600 | tf_op jit(solution)/shard_map/ppermute | solution.py:14
  50.3 255.8 %all-reduce.2.cloned.1.call-done = bf16[1,256,4096]{1,0,2:T(2,128)(2,1)} async-done(((bf16[1,256,4096]{1,0,2:T(2,128)(2,1)}), bf16[1,256,4096]{1,0,2:T(2,128)(2,1)}) %all-reduce.2.cloned.1.call-update) | async-done | bytes 2097168 | tf_op jit(solution)/shard_map/psum | solution.py:19
  306.6 22.9 %reduce = bf16[4096,256]{1,0:T(8,128)(2,1)} reduce(bf16[4096,1,256]{2,1,0:T(2,128)(2,1)} %bitcast.138, bf16[]{:T(256)} %broadcast.237), dimensions={1}, to_apply=%bitcast.84.reduce_sub_computation | reduce | bytes 4194306
  329.5 5.8 %reshape.260 = bf16[8,2,65536]{2,1,0:T(2,128)(2,1)} reshape(bf16[4096,256]{1,0:T(8,128)(2,1)} %reduce) | data formatting | bytes 4194304
  335.3 4.3 all-to-all-start
  346.1 3.2 copy.60
  349.3 21.1 %all-to-all-done = bf16[8,2,65536]{2,1,0:T(2,128)(2,1)} async-done(((bf16[8,2,65536]{2,1,0:T(2,128)(2,1)}), bf16[8,2,65536]{2,1,0:T(2,128)(2,1)}, u32[]{:S(2)}, u32[]{:S(2)}) %all-to-all-start) | async-done | bytes 2097184 | tf_op jit(solution)/shard_map/all_to_all | solution.py:61
  370.5 6.8 %reshape.261 = bf16[4096,1,256]{2,1,0:T(2,128)(2,1)} reshape(bf16[8,2,65536]{2,1,0:T(2,128)(2,1)} %all-to-all-done) | data formatting | bytes 4194304
  382.3 4.2 reshape.250
  391.9 122.3 %while.13 = (s32[]{:T(128)}, bf16[3,512,512]{2,1,0:T(8,128)(2,1)}, s32[3]{0:T(128)S(1)}, s32[]{:T(128)}, bf16[2,2560,2,128]{3,1,2,0:T(8,128)(2,1)S(1)}, /*index=...) while((s32[]{:T(128)}, bf16[3,512,512]{2,1,0:T(8,128)(2,1)}, ...), condition=%wide.region_8.9_spmd, body=%wide.region_3.8_spmd.sunk | while | flops 3808170496 | bytes 132267352 | solution.py:111
  397.7 8.2 %bitcast_reduce_fusion.2 = (f32[2,2,512]{2,1,0:T(2,128)S(1)}, f32[2,512,2,2048]{3,1,2,0:T(8,128)}) fusion(bf16[512,2,2,128]{0,3,2,1:T(8,128)(2,1)S(1)} %bitcast.128, bf16[2048,2,128]{2,0,1:T(8,128)(2,1)S(1)} %copy-done.2), kind=kOutput, calls=%fused_computation.1.clone.1 | convolution fusion | flops 1077934080 | bytes 18358272 | tf_op jit(solution)/shard_map/while/body/eval_jaxpr/ikgd,tkd->kgit/dot_general | solution.py:85
  405.9 4.0 fusion.63
  412.1 8.1 %fusion.65 = f32[2,2,512]{2,1,0:T(2,128)S(1)} fusion(f32[2,512,2,2048]{3,1,2,0:T(8,128)} %get-tuple-element.257, f32[2,2,512]{2,1,0:T(2,128)S(1)} %max.12), kind=kLoop, calls=%fused_computation.3.clone.1 | loop fusion | flops 8386560 | bytes 16793600 | tf_op jit(solution)/shard_map/while/body/eval_jaxpr/reduce_sum | solution.py:91
  420.3 9.5 %fusion.66 = bf16[512,2,2,128]{0,3,2,1:T(8,128)(2,1)S(1)} fusion(f32[2,2,512,128]{2,3,1,0:T(8,128)} %fusion.63, f32[2,512,2,2048]{3,1,2,0:T(8,128)} %get-tuple-element.257, f32[2,2,512]{2,1,0:T(2,128)S(1)} %max.12, bf16[2048,2,128]{0,2,1:T(8,128)(2,1)} %get-tuple-element.291, f32[512,2,2]{0,2,1:T(2,128)S(1)} %add_bitcast_fusion.2), kind=kOutput, calls=%fused_computation.20.clone.1 | convolution fusion | flops 1082916864 | bytes 19415040 | tf_op jit(solution)/shard_map/while/body/eval_jaxpr/kgit,tkd->kgid/dot_general | solution.py:98
  438.5 8.2 %bitcast_reduce_fusion.2 = (f32[2,2,512]{2,1,0:T(2,128)S(1)}, f32[2,512,2,2048]{3,1,2,0:T(8,128)}) fusion(bf16[512,2,2,128]{0,3,2,1:T(8,128)(2,1)S(1)} %bitcast.128, bf16[2048,2,128]{2,0,1:T(8,128)(2,1)S(1)} %copy-done.2), kind=kOutput, calls=%fused_computation.1.clone.1 | convolution fusion | flops 1077934080 | bytes 18358272 | tf_op jit(solution)/shard_map/while/body/eval_jaxpr/ikgd,tkd->kgit/dot_general | solution.py:85
  446.6 4.0 fusion.63
  452.9 8.1 %fusion.65 = f32[2,2,512]{2,1,0:T(2,128)S(1)} fusion(f32[2,512,2,2048]{3,1,2,0:T(8,128)} %get-tuple-element.257, f32[2,2,512]{2,1,0:T(2,128)S(1)} %max.12), kind=kLoop, calls=%fused_computation.3.clone.1 | loop fusion | flops 8386560 | bytes 16793600 | tf_op jit(solution)/shard_map/while/body/eval_jaxpr/reduce_sum | solution.py:91
  461.0 9.5 %fusion.66 = bf16[512,2,2,128]{0,3,2,1:T(8,128)(2,1)S(1)} fusion(f32[2,2,512,128]{2,3,1,0:T(8,128)} %fusion.63, f32[2,512,2,2048]{3,1,2,0:T(8,128)} %get-tuple-element.257, f32[2,2,512]{2,1,0:T(2,128)S(1)} %max.12, bf16[2048,2,128]{0,2,1:T(8,128)(2,1)} %get-tuple-element.291, f32[512,2,2]{0,2,1:T(2,128)S(1)} %add_bitcast_fusion.2), kind=kOutput, calls=%fused_computation.20.clone.1 | convolution fusion | flops 1082916864 | bytes 19415040 | tf_op jit(solution)/shard_map/while/body/eval_jaxpr/kgit,tkd->kgid/dot_general | solution.py:98
  479.2 8.2 %bitcast_reduce_fusion.2 = (f32[2,2,512]{2,1,0:T(2,128)S(1)}, f32[2,512,2,2048]{3,1,2,0:T(8,128)}) fusion(bf16[512,2,2,128]{0,3,2,1:T(8,128)(2,1)S(1)} %bitcast.128, bf16[2048,2,128]{2,0,1:T(8,128)(2,1)S(1)} %copy-done.2), kind=kOutput, calls=%fused_computation.1.clone.1 | convolution fusion | flops 1077934080 | bytes 18358272 | tf_op jit(solution)/shard_map/while/body/eval_jaxpr/ikgd,tkd->kgit/dot_general | solution.py:85
  487.4 4.0 fusion.63
  493.7 8.1 %fusion.65 = f32[2,2,512]{2,1,0:T(2,128)S(1)} fusion(f32[2,512,2,2048]{3,1,2,0:T(8,128)} %get-tuple-element.257, f32[2,2,512]{2,1,0:T(2,128)S(1)} %max.12), kind=kLoop, calls=%fused_computation.3.clone.1 | loop fusion | flops 8386560 | bytes 16793600 | tf_op jit(solution)/shard_map/while/body/eval_jaxpr/reduce_sum | solution.py:91
  501.8 9.5 %fusion.66 = bf16[512,2,2,128]{0,3,2,1:T(8,128)(2,1)S(1)} fusion(f32[2,2,512,128]{2,3,1,0:T(8,128)} %fusion.63, f32[2,512,2,2048]{3,1,2,0:T(8,128)} %get-tuple-element.257, f32[2,2,512]{2,1,0:T(2,128)S(1)} %max.12, bf16[2048,2,128]{0,2,1:T(8,128)(2,1)} %get-tuple-element.291, f32[512,2,2]{0,2,1:T(2,128)S(1)} %add_bitcast_fusion.2), kind=kOutput, calls=%fused_computation.20.clone.1 | convolution fusion | flops 1082916864 | bytes 19415040 | tf_op jit(solution)/shard_map/while/body/eval_jaxpr/kgit,tkd->kgid/dot_general | solution.py:98
  (103 shorter events, 69.8 us)
Async XLA Ops:
  6.5 299.5 %all-reduce.2.cloned.1.call-start = ((), (), s32[]{:S(2)}) async-start(), calls=%async_computation.1 | async-start | bytes 8388608 | tf_op jit(solution)/shard_map/psum | solution.py:19
  23.4 0.7 copy-start.7
  23.4 0.7 copy-start.6
  23.4 1.2 copy-start.5
  31.6 0.8 copy-start.3
  42.3 8.0 %copy-start.8 = (f32[128]{0:T(128)S(1)}, f32[128]{0:T(128)}, u32[]{:S(2)}) copy-start(f32[128]{0:T(128)} %param.13) | copy-start | bytes 1540
  42.3 300.8 %collective-permute-start = (bf16[2,1536,256]{1,2,0:T(8,128)(2,1)}, bf16[2,1536,256]{1,2,0:T(8,128)(2,1)}, u32[]{:S(2)}, u32[]{:S(2)}) collective-permute-start(bf16[2,1536,256]{1,2,0:T(8,128)(2,1)} %pad_maximum_fusion), channel_id=1, source_target_pairs={{0,8},{8,16},{16,24},{24,32},{32,40},{40,48},{48,56},{56,64},{64,7... | collective-permute-start | bytes 4718600 | tf_op jit(solution)/shard_map/ppermute | solution.py:14
  335.3 35.2 %all-to-all-start = ((bf16[8,2,65536]{2,1,0:T(2,128)(2,1)}), bf16[8,2,65536]{2,1,0:T(2,128)(2,1)}, u32[]{:S(2)}, u32[]{:S(2)}) async-start(bf16[8,2,65536]{2,1,0:T(2,128)(2,1)} %reshape.260), calls=%async_computation | async-start | bytes 4194304 | tf_op jit(solution)/shard_map/all_to_all | solution.py:61
  339.7 1.3 copy-start.4
  391.9 3.8 copy-start
  395.6 2.0 copy-start.2
  420.3 12.4 %copy-start.1 = (bf16[2,2560,2,128]{3,1,2,0:T(8,128)(2,1)S(1)}, bf16[2,2560,2,128]{3,1,2,0:T(8,128)(2,1)}, u32[]{:S(2)}) copy-start(bf16[2,2560,2,128]{3,1,2,0:T(8,128)(2,1)} %copy-done) | copy-start | bytes 7864324 | tf_op jit(solution)/shard_map/while
  432.7 3.8 copy-start
  436.4 2.0 copy-start.2
  461.0 12.4 %copy-start.1 = (bf16[2,2560,2,128]{3,1,2,0:T(8,128)(2,1)S(1)}, bf16[2,2560,2,128]{3,1,2,0:T(8,128)(2,1)}, u32[]{:S(2)}) copy-start(bf16[2,2560,2,128]{3,1,2,0:T(8,128)(2,1)} %copy-done) | copy-start | bytes 7864324 | tf_op jit(solution)/shard_map/while
  473.4 3.8 copy-start
  477.2 2.0 copy-start.2
  501.8 12.4 %copy-start.1 = (bf16[2,2560,2,128]{3,1,2,0:T(8,128)(2,1)S(1)}, bf16[2,2560,2,128]{3,1,2,0:T(8,128)(2,1)}, u32[]{:S(2)}) copy-start(bf16[2,2560,2,128]{3,1,2,0:T(8,128)(2,1)} %copy-done) | copy-start | bytes 7864324 | tf_op jit(solution)/shard_map/while
Sparse Core Ops, SparseCore 0:
  23.5 282.4 all-reduce.1
where the time goes:
time: 523 us; the launch traced here: 521 us
  waiting for transfers between devices  277 us (53%)
  other arithmetic  82.9 us (16%)
  matrix products  71.1 us (14%)
  local copies, waits for them, and re-layouts  64.3 us (12%)
  between operations  14.2 us (3%)
  starting transfers between devices  9.58 us (2%)
    psum x1, waiting for transfers between devices, spread(): return lax.psum(jnp.where(mine, array, jnp.zeros_like(array)), axis)  256 us
    reduce_sum x6, other arithmetic, one_block(): total = jnp.sum(exp_band, axis=-1) + jnp.sum(exp_pre, axis=-1)  31.1 us
    unnamed x19, local copies, waits for them, and re-layouts  30.5 us
    dot_general x3, matrix products, one_block(): jnp.einsum('kgit,tkd->kgid', exp_pre.astype(jnp.bfloat16), prefix_value,...  28.5 us
    dot_general x3, matrix products, one_block(): jnp.einsum('ikgd,tkd->kgit', query_block, prefix_key, preferred_element_t...  24.5 us
    unnamed x1, other arithmetic  22.9 us
    all_to_all x1, waiting for transfers between devices, on_device(): mine = lax.all_to_all(slab, 'head', split_axis=2, concat_axis=1, tiled=True)  21.1 us
    dot_general x3, matrix products, one_block(): jnp.einsum('kgij,jkd->kgid', exp_band.astype(jnp.bfloat16), value_block,...  12 us
  transfers between devices with their start and end apart: 3, of which 2 were waited for; matrix products, arithmetic and copies ran while one was open for 11% of the time, Pallas kernels for 0%

commit v1 on v0

v1 whole, which is shorter than its diff:
```python
import functools

import jax
import jax.numpy as jnp
from jax import lax
from jax.experimental import pallas as pl
from jax.experimental.pallas import tpu as pltpu
from jax.sharding import PartitionSpec as P

HD = 128
WINDOW = 1024
QSCALAR = 168
YH, NZ, NC = 2, 8, 2
TILE = 256
NEG = -1e30
VMEM_LIMIT = 56 * 1024 * 1024


def where_is(i):
    return i // (NZ * NC), (i // NC) % NZ, i % NC


def hop(array, move):
    route = []
    for i in range(YH * NZ * NC):
        y, z, c = move(*where_is(i))
        route.append((i, (y * NZ + z) * NC + c))
    return lax.ppermute(array, "seq", route)


def other_core(array):
    return hop(array, lambda y, z, c: (y, z, 1 - c))


def other_half(array):
    return hop(array, lambda y, z, c: (1 - y, z, c))


def round_z(array, r):
    return hop(array, lambda y, z, c: (y, (z + r) % NZ, c))


ROUNDS = (4, 3, 5, 2, 6, 1, 7)


def pick(array, at):
    return lax.dynamic_index_in_dim(array, at, 0, keepdims=False)


def scatter_from(slab, root):
    me = lax.axis_index("seq")
    y, z, c = where_is(me)
    root_y, root_z, root_c = where_is(root)
    rows, columns = slab.shape
    part = slab.reshape(NC, rows // NC, columns)
    came = other_core(pick(part, 1 - c))
    part = jnp.where(root_c == c, pick(part, c), came)
    part = part.reshape(YH, -1, columns)
    came = other_half(pick(part, 1 - y))
    part = jnp.where(root_y == y, pick(part, y), came)
    part = part.reshape(NZ, -1, columns)
    kept = pick(part, z)
    for r in ROUNDS:
        came = round_z(pick(part, (z + r) % NZ), r)
        kept = jnp.where(root_z == (z - r) % NZ, came, kept)
    return kept


def normed(rows, gain, cosine, sine):
    mean_sq = jnp.mean(rows * rows, axis=-1, keepdims=True)
    rows = rows * lax.rsqrt(mean_sq + 1e-06) * gain
    return rows * cosine + pltpu.roll(rows, HD // 2, 1) * sine


def dot_t(a, b):
    return lax.dot_general(a, b, (((1,), (1,)), ((), ())), preferred_element_type=jnp.float32)


def pack_state(parts):
    lane = lax.broadcasted_iota(jnp.int32, (TILE, HD), 1)
    packed = jnp.zeros((TILE, HD), jnp.float32)
    for at, part in enumerate(parts):
        packed = jnp.where(lane == at, part, packed)
    return packed


def band_kernel(
    first_ref, q_ref, kh_ref, k_ref, vh_ref, v_ref, qg_ref, kg_ref, cos_ref, sin_ref,
    qn_ref, acc_ref, ml_ref, kn_ref, va_ref,
):
    local = q_ref.shape[0]
    local_kv = k_ref.shape[1] // HD
    group = q_ref.shape[1] // HD // local_kv
    ones = jnp.ones((WINDOW, HD), jnp.bfloat16)
    for c in range(local_kv):
        columns = slice(c * HD, (c + 1) * HD)
        va_ref[:WINDOW, 2 * c * HD : (2 * c + 1) * HD] = vh_ref[:, columns]
        va_ref[WINDOW:, 2 * c * HD : (2 * c + 1) * HD] = v_ref[:, columns]
        va_ref[:WINDOW, (2 * c + 1) * HD : (2 * c + 2) * HD] = ones
        va_ref[WINDOW:, (2 * c + 1) * HD : (2 * c + 2) * HD] = jnp.ones((local, HD), jnp.bfloat16)

    def halo(t, _):
        at = pl.ds(pl.multiple_of(t * TILE, TILE), TILE)
        for c in range(local_kv):
            columns = slice(c * HD, (c + 1) * HD)
            rows = kh_ref[at, columns].astype(jnp.float32)
            kn_ref[at, columns] = normed(rows, kg_ref[...], cos_ref[at, :], sin_ref[at, :]).astype(jnp.bfloat16)
        return 0

    lax.fori_loop(0, WINDOW // TILE, halo, 0)

    def own(t, _):
        at = pl.ds(pl.multiple_of(t * TILE, TILE), TILE)
        to = pl.ds(pl.multiple_of(t * TILE + WINDOW, TILE), TILE)
        cosine, sine = cos_ref[to, :], sin_ref[to, :]
        for c in range(local_kv):
            columns = slice(c * HD, (c + 1) * HD)
            rows = k_ref[at, columns].astype(jnp.float32)
            kn_ref[to, columns] = normed(rows, kg_ref[...], cosine, sine).astype(jnp.bfloat16)
        for h in range(local_kv * group):
            columns = slice(h * HD, (h + 1) * HD)
            rows = q_ref[at, columns].astype(jnp.float32)
            rows = normed(rows, qg_ref[...], cosine, sine) * QSCALAR ** (-0.5)
            qn_ref[at, columns] = rows.astype(jnp.bfloat16)
        return 0

    lax.fori_loop(0, local // TILE, own, 0)

    span = WINDOW + TILE
    rows_in = lax.broadcasted_iota(jnp.int32, (group * TILE, TILE), 0) % TILE
    columns_in = lax.broadcasted_iota(jnp.int32, (group * TILE, TILE), 1)
    early = columns_in > rows_in
    late = columns_in <= rows_in
    lowest = jnp.where(first_ref[0] == 1, WINDOW, 0)

    def band(t, _):
        at = pl.ds(pl.multiple_of(t * TILE, TILE), TILE)
        keys_at = pl.ds(pl.multiple_of(t * TILE, TILE), span)
        column = lax.broadcasted_iota(jnp.int32, (1, span), 1) + t * TILE
        bias = jnp.where(column >= lowest, 0.0, NEG)
        tops, totals = [], []
        for c in range(local_kv):
            heads = [slice((c * group + g) * HD, (c * group + g + 1) * HD) for g in range(group)]
            query = jnp.concatenate([qn_ref[at, h] for h in heads], axis=0)
            score = dot_t(query, kn_ref[keys_at, c * HD : (c + 1) * HD]) + bias
            score = jnp.concatenate(
                [
                    jnp.where(early, score[:, :TILE], NEG),
                    score[:, TILE:WINDOW],
                    jnp.where(late, score[:, WINDOW:], NEG),
                ],
                axis=1,
            )
            top = jnp.max(score, axis=1, keepdims=True)
            weight = jnp.exp(score - top).astype(jnp.bfloat16)
            out = jnp.dot(
                weight,
                va_ref[keys_at, 2 * c * HD : (2 * c + 2) * HD],
                preferred_element_type=jnp.float32,
            )
            for g, h in enumerate(heads):
                mine = slice(g * TILE, (g + 1) * TILE)
                acc_ref[at, h] = out[mine, :HD]
                tops.append(top[mine])
                totals.append(out[mine, HD:])
        ml_ref[at, :] = pack_state(tops + totals)
        return 0

    lax.fori_loop(0, local // TILE, band, 0)


def prefix_kernel(last, q_ref, acc_in_ref, ml_in_ref, p_ref, *rest):
    if last:
        out_ref, va_ref = rest
    else:
        acc_ref, ml_ref, va_ref = rest
    local = q_ref.shape[0]
    local_kv = p_ref.shape[1] // (2 * HD)
    group = q_ref.shape[1] // HD // local_kv
    tokens = p_ref.shape[0]
    for c in range(local_kv):
        va_ref[:, 2 * c * HD : (2 * c + 1) * HD] = p_ref[:, (2 * c + 1) * HD : (2 * c + 2) * HD]
        va_ref[:, (2 * c + 1) * HD : (2 * c + 2) * HD] = jnp.ones((tokens, HD), jnp.bfloat16)

    def step(t, _):
        at = pl.ds(pl.multiple_of(t * TILE, TILE), TILE)
        state = ml_in_ref[at, :]
        count = local_kv * group
        tops, totals = [], []
        for c in range(local_kv):
            heads = [slice((c * group + g) * HD, (c * group + g + 1) * HD) for g in range(group)]
            query = jnp.concatenate([q_ref[at, h] for h in heads], axis=0)
            before = jnp.concatenate(
                [state[:, c * group + g : c * group + g + 1] for g in range(group)], axis=0
            )
            score = dot_t(query, p_ref[:, 2 * c * HD : (2 * c + 1) * HD])
            top = jnp.maximum(before, jnp.max(score, axis=1, keepdims=True))
            weight = jnp.exp(score - top).astype(jnp.bfloat16)
            out = jnp.dot(
                weight, va_ref[:, 2 * c * HD : (2 * c + 2) * HD], preferred_element_type=jnp.float32
            )
            keep = jnp.exp(before - top)
            for g, h in enumerate(heads):
                mine = slice(g * TILE, (g + 1) * TILE)
                at_head = count + c * group + g
                total = state[:, at_head : at_head + 1] * keep[mine] + out[mine, HD:]
                summed = acc_in_ref[at, h] * keep[mine] + out[mine, :HD]
                if last:
                    out_ref[at, h] = (summed / total).astype(jnp.bfloat16)
                else:
                    acc_ref[at, h] = summed
                    tops.append(top[mine])
                    totals.append(total)
        if not last:
            ml_ref[at, :] = pack_state(tops + totals)
        return 0

    lax.fori_loop(0, local // TILE, step, 0)


WHOLE = pl.BlockSpec(memory_space=pltpu.VMEM)
PARAMS = pltpu.CompilerParams(vmem_limit_bytes=VMEM_LIMIT)


def cost(pairs, in_out):
    return pl.CostEstimate(flops=4 * pairs * HD, transcendentals=pairs, bytes_accessed=in_out)


def band_part(first, q, kh, k, vh, v, q_gain, k_gain, cosine, sine):
    local, width = q.shape
    return pl.pallas_call(
        band_kernel,
        out_shape=(
            jax.ShapeDtypeStruct((local, width), jnp.bfloat16),
            jax.ShapeDtypeStruct((local, width), jnp.float32),
            jax.ShapeDtypeStruct((local, HD), jnp.float32),
        ),
        in_specs=[pl.BlockSpec(memory_space=pltpu.SMEM)] + [WHOLE] * 9,
        out_specs=(WHOLE,) * 3,
        scratch_shapes=[
            pltpu.VMEM((WINDOW + local, k.shape[1]), jnp.bfloat16),
            pltpu.VMEM((WINDOW + local, 2 * k.shape[1]), jnp.bfloat16),
        ],
        compiler_params=PARAMS,
        cost_estimate=cost(local * (width // HD) * (WINDOW + TILE), 12 << 20),
        name="band",
    )(first, q, kh, k, vh, v, q_gain, k_gain, cosine, sine)


def prefix_part(last, q, acc, ml, piece):
    local, width = q.shape
    if last:
        out_shape = jax.ShapeDtypeStruct((local, width), jnp.bfloat16)
        out_specs = WHOLE
    else:
        out_shape = (
            jax.ShapeDtypeStruct((local, width), jnp.float32),
            jax.ShapeDtypeStruct((local, HD), jnp.float32),
        )
        out_specs = (WHOLE,) * 2
    return pl.pallas_call(
        functools.partial(prefix_kernel, last),
        out_shape=out_shape,
        in_specs=[WHOLE] * 4,
        out_specs=out_specs,
        scratch_shapes=[pltpu.VMEM(piece.shape, jnp.bfloat16)],
        compiler_params=PARAMS,
        cost_estimate=cost(local * (width // HD) * piece.shape[0], 12 << 20),
        name="prefix_last" if last else "prefix",
    )(q, acc, ml, piece)


def on_device(queries, keys, values, q_gain, k_gain, positions, prefix_cache, owner):
    local = queries.shape[0]
    seq = lax.axis_index("seq")
    onward = [(i, i + 1) for i in range(lax.axis_size("seq") - 1)]
    keys_before = lax.ppermute(keys[local - WINDOW :], "seq", onward)
    values_before = lax.ppermute(values[local - WINDOW :], "seq", onward)

    mine = scatter_from(prefix_cache[0], owner[0])
    width = mine.shape[1] // lax.axis_size("head")
    mine = lax.all_to_all(mine, "head", split_axis=1, concat_axis=0, tiled=True)
    pieces = [mine] + [round_z(mine, r) for r in ROUNDS]
    gathered = jnp.concatenate(pieces, axis=0)
    gathered = jnp.concatenate([gathered, other_half(gathered)], axis=0)
    sibling = other_core(gathered)

    half = HD // 2
    freq = 10000.0 ** (-(jnp.arange(half).astype(jnp.float32) * 2.0) / HD)
    extended = positions[0] + jnp.arange(-WINDOW, local, dtype=jnp.int32)
    angle = extended.astype(jnp.float32)[:, None] * freq[None, :]
    cosine, sine = jnp.cos(angle), jnp.sin(angle)
    cosine = jnp.concatenate([cosine, cosine], axis=1)
    sine = jnp.concatenate([-sine, sine], axis=1)
    first = (seq == 0).astype(jnp.int32).reshape(1)
    query, acc, ml = band_part(
        first, queries, keys_before, keys, values_before, values,
        (1.0 + q_gain)[None], (1.0 + k_gain)[None], cosine, sine,
    )
    acc, ml = prefix_part(False, query, acc, ml, gathered)
    return prefix_part(True, query, acc, ml, sibling)


def solution(mesh):
    return jax.shard_map(
        on_device,
        mesh=mesh,
        in_specs=(
            P("seq", "head"),
            P("seq", "head"),
            P("seq", "head"),
            P(),
            P(),
            P("seq"),
            P("seq", "head", None),
            P(),
        ),
        out_specs=P("seq", "head"),
        check_vma=False,
    )
```

time: 523 us -> 165 us (0.32)
  waiting for transfers between devices: 277 us -> 27.4 us
  other arithmetic: 82.9 us -> 10.2 us
  matrix products: 71.1 us -> 0 us
  Pallas kernels: 0 us -> 63.8 us
  local copies, waits for them, and re-layouts: 64.3 us -> 5.95 us
  starting transfers between devices: 9.58 us -> 54.8 us
  between operations: 14.2 us -> 0.93 us
    psum x1 -> x0, waiting for transfers between devices: 256 us -> none  [spread(): return lax.psum(jnp.where(mine, array, jnp.zeros_like(array)), axis)]
    dot_general x12 -> x0, matrix products: 71.1 us -> none  [the longest x3 28.5 us: one_block(): jnp.einsum('kgit,tkd->kgid', exp_pre.astype(jnp.bfloat16), prefix_value,...]
    pallas_call x0 -> x3, Pallas kernels: none -> 63.8 us  [the longest x2 37.2 us: prefix_part(): pl.pallas_call(functools.partial(prefix_kernel, last), out_shape=out_shap...]
    ppermute x1 -> x20, starting transfers between devices: 5.24 us -> 49.8 us  [the longest x18 42.7 us: hop(): return lax.ppermute(array, 'seq', route)]
    reduce_sum x8 -> x0, other arithmetic: 34.1 us -> none  [the longest x6 31.1 us: one_block(): total = jnp.sum(exp_band, axis=-1) + jnp.sum(exp_pre, axis=-1)]
    unnamed x19 -> x23, local copies, waits for them, and re-layouts: 30.5 us -> 2.06 us
    unnamed x1 -> x0, other arithmetic: 22.9 us -> none
    ppermute x1 -> x20, waiting for transfers between devices: 0.01 us -> 21.9 us  [the longest x18 21.9 us: hop(): return lax.ppermute(array, 'seq', route)]
  transfers between devices with their start and end apart: 3 -> 21, of which waited for: 2 -> 6; matrix products, arithmetic and copies ran while one was open for 11% -> 7% of each run, Pallas kernels for 0% -> 28%
where the time goes in v1:
time: 165 us; the launch traced here: 163 us
  Pallas kernels  63.8 us (39%)
  starting transfers between devices  54.8 us (33%)
  waiting for transfers between devices  27.4 us (17%)
  other arithmetic  10.2 us (6%)
  local copies, waits for them, and re-layouts  5.95 us (4%)
    ppermute x18, starting transfers between devices, hop(): return lax.ppermute(array, 'seq', route)  42.7 us
    pallas_call x2, Pallas kernels, prefix_part(): pl.pallas_call(functools.partial(prefix_kernel, last), out_shape=out_shap...  37.2 us
    pallas_call x1, Pallas kernels, band_part(): pl.pallas_call(band_kernel, out_shape=(jax.ShapeDtypeStruct((local, width...  26.6 us
    ppermute x18, waiting for transfers between devices, hop(): return lax.ppermute(array, 'seq', route)  21.9 us
    all_to_all x1, waiting for transfers between devices, on_device(): mine = lax.all_to_all(mine, 'head', split_axis=1, concat_axis=0, tiled=True)  5.55 us
    ppermute x1, starting transfers between devices, on_device(): keys_before = lax.ppermute(keys[local - WINDOW:], 'seq', onward)  5.21 us
    all_to_all x1, starting transfers between devices, on_device(): mine = lax.all_to_all(mine, 'head', split_axis=1, concat_axis=0, tiled=True)  5.03 us
    neg x1, other arithmetic, on_device(): sine = jnp.concatenate([-sine, sine], axis=1)  4.63 us
  transfers between devices with their start and end apart: 21, of which 6 were waited for; matrix products, arithmetic and copies ran while one was open for 7% of the time, Pallas kernels for 28%

profile of v1, /device:TPU:1, one launch (start us, length us, event | category | flops | bytes accessed | tf_op | source)
XLA Modules:
  0.0 163.1 jit_solution(1412391168281538425)
XLA Ops:
  1.4 3.3 %collective-permute-start.2 = (bf16[128,4096]{1,0:T(8,128)(2,1)S(1)}, bf16[128,4096]{1,0:T(8,128)(2,1)}, u32[]{:S(2)}, u32[]{:S(2)}) collective-permute-start(bf16[128,4096]{1,0:T(8,128)(2,1)S(1)} %dynamic-slice_bitcast_fusion), channel_id=1, source_target_pairs={{0,8},{8,0},{16,24},{24,16},{32,40},{40,32},{48,56},{56,48},{64,72... | collective-permute-start | bytes 3145736 | tf_op jit(solution)/shard_map/ppermute | solution.py:28
  5.5 1.7 %collective-permute-done.2 = bf16[128,4096]{1,0:T(8,128)(2,1)} collective-permute-done((bf16[128,4096]{1,0:T(8,128)(2,1)S(1)}, bf16[128,4096]{1,0:T(8,128)(2,1)}, u32[]{:S(2)}, u32[]{:S(2)}) %collective-permute-start.2) | collective-permute-done | bytes 1048608 | tf_op jit(solution)/shard_map/ppermute | solution.py:28
  9.9 13.6 %collective-permute-done.3 = bf16[64,4096]{1,0:T(8,128)(2,1)S(1)} collective-permute-done((bf16[64,4096]{1,0:T(8,128)(2,1)S(1)}, bf16[64,4096]{1,0:T(8,128)(2,1)S(1)}, u32[]{:S(2)}, u32[]{:S(2)}) %collective-permute-start.3) | collective-permute-done | bytes 524320 | tf_op jit(solution)/shard_map/ppermute | solution.py:28
  23.6 5.3 %collective-permute-start.10 = (bf16[8,4096]{1,0:T(8,128)(2,1)S(1)}, bf16[8,4096]{1,0:T(8,128)(2,1)S(1)}, u32[]{:S(2)}, u32[]{:S(2)}) collective-permute-start(bf16[8,4096]{1,0:T(8,128)(2,1)S(1)} %get-tuple-element.15), channel_id=1, source_target_pairs={{0,64},{8,72},{16,80},{24,88},{32,96},{40,104},{48,112},{56,120},{... | collective-permute-start | bytes 196616 | tf_op jit(solution)/shard_map/ppermute | solution.py:28
  33.3 2.4 %collective-permute-start.7 = (bf16[8,4096]{1,0:T(8,128)(2,1)S(1)}, bf16[8,4096]{1,0:T(8,128)(2,1)S(1)}, u32[]{:S(2)}, u32[]{:S(2)}) collective-permute-start(bf16[8,4096]{1,0:T(8,128)(2,1)S(1)} %get-tuple-element.18), channel_id=1, source_target_pairs={{0,32},{8,40},{16,48},{24,56},{32,64},{40,72},{48,80},{56,88},{64,... | collective-permute-start | bytes 196616 | tf_op jit(solution)/shard_map/ppermute | solution.py:28
  35.6 2.9 %collective-permute-start.8 = (bf16[8,4096]{1,0:T(8,128)(2,1)S(1)}, bf16[8,4096]{1,0:T(8,128)(2,1)S(1)}, u32[]{:S(2)}, u32[]{:S(2)}) collective-permute-start(bf16[8,4096]{1,0:T(8,128)(2,1)S(1)} %get-tuple-element.17), channel_id=1, source_target_pairs={{0,80},{8,88},{16,96},{24,104},{32,112},{40,120},{48,0},{56,8},{64... | collective-permute-start | bytes 196616 | tf_op jit(solution)/shard_map/ppermute | solution.py:28
  40.5 5.2 %collective-permute-start = (bf16[1024,256]{1,0:T(8,128)(2,1)S(1)}, bf16[1024,256]{1,0:T(8,128)(2,1)S(1)}, u32[]{:S(2)}, u32[]{:S(2)}) collective-permute-start(bf16[1024,256]{1,0:T(8,128)(2,1)S(1)} %slice.9), channel_id=1, source_target_pairs={{0,8},{8,16},{16,24},{24,32},{32,40},{40,48},{48,56},{56,64},{64,7... | collective-permute-start | bytes 1572872 | tf_op jit(solution)/shard_map/ppermute | solution.py:277
  45.7 1.9 %collective-permute-start.1 = (bf16[1024,256]{1,0:T(8,128)(2,1)S(1)}, bf16[1024,256]{1,0:T(8,128)(2,1)S(1)}, u32[]{:S(2)}, u32[]{:S(2)}) collective-permute-start(bf16[1024,256]{1,0:T(8,128)(2,1)S(1)} %slice.10), channel_id=1, source_target_pairs={{0,8},{8,16},{16,24},{24,32},{32,40},{40,48},{48,56},{56,64},{64,7... | collective-permute-start | bytes 1572872 | tf_op jit(solution)/shard_map/ppermute | solution.py:278
  48.3 5.0 %all-to-all-start = ((bf16[8,8,512]{2,0,1:T(8,128)(2,1)}), bf16[8,8,512]{2,0,1:T(8,128)(2,1)S(1)}, u32[]{:S(2)}, u32[]{:S(2)}) async-start(bf16[8,8,512]{2,0,1:T(8,128)(2,1)} %bitcast.20), calls=%async_computation | async-start | bytes 131072 | tf_op jit(solution)/shard_map/all_to_all | solution.py:282
  53.4 5.5 %all-to-all-done = bf16[8,8,512]{2,0,1:T(8,128)(2,1)S(1)} async-done(((bf16[8,8,512]{2,0,1:T(8,128)(2,1)}), bf16[8,8,512]{2,0,1:T(8,128)(2,1)S(1)}, u32[]{:S(2)}, u32[]{:S(2)}) %all-to-all-start) | async-done | bytes 65568 | tf_op jit(solution)/shard_map/all_to_all | solution.py:282
  58.9 2.7 %collective-permute-start.11 = (bf16[64,512]{1,0:T(8,128)(2,1)S(1)}, bf16[64,512]{1,0:T(8,128)(2,1)S(1)}, u32[]{:S(2)}, u32[]{:S(2)}) collective-permute-start(bf16[64,512]{1,0:T(8,128)(2,1)S(1)} %bitcast.63), channel_id=1, source_target_pairs={{0,64},{8,72},{16,80},{24,88},{32,96},{40,104},{48,112},{56,120},{... | collective-permute-start | bytes 196616 | tf_op jit(solution)/shard_map/ppermute | solution.py:28
  61.6 2.9 %collective-permute-start.12 = (bf16[64,512]{1,0:T(8,128)(2,1)S(1)}, bf16[64,512]{1,0:T(8,128)(2,1)S(1)}, u32[]{:S(2)}, u32[]{:S(2)}) collective-permute-start(bf16[64,512]{1,0:T(8,128)(2,1)S(1)} %bitcast.64), channel_id=1, source_target_pairs={{0,48},{8,56},{16,64},{24,72},{32,80},{40,88},{48,96},{56,104},{64... | collective-permute-start | bytes 196616 | tf_op jit(solution)/shard_map/ppermute | solution.py:28
  66.1 3.7 %collective-permute-start.14 = (bf16[64,512]{1,0:T(8,128)(2,1)S(1)}, bf16[64,512]{1,0:T(8,128)(2,1)S(1)}, u32[]{:S(2)}, u32[]{:S(2)}) collective-permute-start(bf16[64,512]{1,0:T(8,128)(2,1)S(1)} %bitcast.66), channel_id=1, source_target_pairs={{0,32},{8,40},{16,48},{24,56},{32,64},{40,72},{48,80},{56,88},{64,... | collective-permute-start | bytes 196616 | tf_op jit(solution)/shard_map/ppermute | solution.py:28
  69.8 2.8 %collective-permute-start.15 = (bf16[64,512]{1,0:T(8,128)(2,1)S(1)}, bf16[64,512]{1,0:T(8,128)(2,1)S(1)}, u32[]{:S(2)}, u32[]{:S(2)}) collective-permute-start(bf16[64,512]{1,0:T(8,128)(2,1)S(1)} %bitcast.67), channel_id=1, source_target_pairs={{0,96},{8,104},{16,112},{24,120},{32,0},{40,8},{48,16},{56,24},{64... | collective-permute-start | bytes 196616 | tf_op jit(solution)/shard_map/ppermute | solution.py:28
  73.3 2.5 %collective-permute-start.17 = (bf16[64,512]{1,0:T(8,128)(2,1)S(1)}, bf16[64,512]{1,0:T(8,128)(2,1)S(1)}, u32[]{:S(2)}, u32[]{:S(2)}) collective-permute-start(bf16[64,512]{1,0:T(8,128)(2,1)S(1)} %bitcast.69), channel_id=1, source_target_pairs={{0,112},{8,120},{16,0},{24,8},{32,16},{40,24},{48,32},{56,40},{64,... | collective-permute-start | bytes 196616 | tf_op jit(solution)/shard_map/ppermute | solution.py:28
  75.7 2.0 %collective-permute-done.15 = bf16[64,512]{1,0:T(8,128)(2,1)S(1)} collective-permute-done((bf16[64,512]{1,0:T(8,128)(2,1)S(1)}, bf16[64,512]{1,0:T(8,128)(2,1)S(1)}, u32[]{:S(2)}, u32[]{:S(2)}) %collective-permute-start.15) | collective-permute-done | bytes 65568 | tf_op jit(solution)/shard_map/ppermute | solution.py:28
  78.8 2.0 %collective-permute-start.18 = (bf16[512,512]{1,0:T(8,128)(2,1)S(1)}, bf16[512,512]{1,0:T(8,128)(2,1)S(1)}, u32[]{:S(2)}, u32[]{:S(2)}) collective-permute-start(bf16[512,512]{1,0:T(8,128)(2,1)S(1)} %get-tuple-element.22), channel_id=1, source_target_pairs={{0,128},{8,136},{16,144},{24,152},{32,160},{40,168},{48,176},{56,1... | collective-permute-start | bytes 1572872 | tf_op jit(solution)/shard_map/ppermute | solution.py:28
  80.8 4.6 %fusion.1 = (f32[2560,64]{1,0:T(8,128)S(1)}, f32[2560,64]{1,0:T(8,128)S(1)}, f32[2560,64]{1,0:T(8,128)S(1)}) fusion(f32[64]{0:T(128)S(1)} %multiply_power_fusion, f32[2560]{0:T(1024)S(1)} %add_convert_fusion), kind=kLoop, calls=%fused_computation.9 | loop fusion | flops 327680 | bytes 1976576 | tf_op jit(solution)/shard_map/neg | solution.py:294
  85.4 3.6 %collective-permute-done.18 = bf16[512,512]{1,0:T(8,128)(2,1)S(1)} collective-permute-done((bf16[512,512]{1,0:T(8,128)(2,1)S(1)}, bf16[512,512]{1,0:T(8,128)(2,1)S(1)}, u32[]{:S(2)}, u32[]{:S(2)}) %collective-permute-start.18) | collective-permute-done | bytes 524320 | tf_op jit(solution)/shard_map/ppermute | solution.py:28
  89.0 6.0 %collective-permute-start.19 = (bf16[1024,512]{1,0:T(8,128)(2,1)S(1)}, bf16[1024,512]{1,0:T(8,128)(2,1)S(1)}, u32[]{:S(2)}, u32[]{:S(2)}) collective-permute-start(bf16[1024,512]{1,0:T(8,128)(2,1)S(1)} %constant_dynamic-update-slice_fusion.8.p_ref), channel_id=1, source_target_pairs={{0,8},{8,0},{16,24},{24,16},{32,40},{40,32},{48,56},{56,48},{64,72... | collective-permute-start | bytes 3145736 | tf_op jit(solution)/shard_map/ppermute | solution.py:28
  95.0 2.2 %pad_maximum_fusion = (f32[2560,128]{1,0:T(8,128)}, f32[2560,128]{1,0:T(8,128)}) fusion(f32[2560,64]{1,0:T(8,128)S(1)} %get-tuple-element.40, f32[2560,64]{1,0:T(8,128)S(1)} %get-tuple-element.39, f32[2560,64]{1,0:T(8,128)S(1)} %get-tuple-element.38), kind=kLoop, calls=%fused_computation.2 | loop fusion | flops 655360 | bytes 4587520 | tf_op jit(solution)/shard_map/concatenate | solution.py:293
  98.3 26.6 %band.1 = (bf16[1536,512]{1,0:T(8,128)(2,1)}, f32[1536,512]{1,0:T(8,128)}, f32[1536,128]{1,0:T(8,128)}) custom-call(s32[1]{0:T(128)} %bitcast.first_ref, bf16[1536,512]{1,0:T(8,128)(2,1)} %q_ref.1, bf16[1024,256]{1,0:T(8,128)(2,1)} %copy-done.6, bf16[1536,256]{1,0:T(8,128)(2,1)} %k_ref.1, bf16[1024,256]{1,0:T(8,128)(2,1)} %copy-done.7, ...), custom_call_target="tpu_custom_call" | custom-call | flops 4026531840 | bytes 12582912 | tf_op jit(solution)/shard_map/band/pallas_call | solution.py:231
  124.9 19.0 %prefix.1 = (f32[1536,512]{1,0:T(8,128)}, f32[1536,128]{1,0:T(8,128)}) custom-call(bf16[1536,512]{1,0:T(8,128)(2,1)} %get-tuple-element.10.q_ref, f32[1536,512]{1,0:T(8,128)} %get-tuple-element.11.acc_in_ref, f32[1536,128]{1,0:T(8,128)} %get-tuple-element.12.ml_in_ref, bf16[1024,512]{1,0:T(8,128)(2,1)} %copy-done.2), custom_call_target="tpu_custom_call" | custom-call | flops 3221225472 | bytes 12582912 | tf_op jit(solution)/shard_map/prefix/pallas_call | solution.py:261
  144.9 18.2 %prefix_last.1 = bf16[1536,512]{1,0:T(8,128)(2,1)} custom-call(bf16[1536,512]{1,0:T(8,128)(2,1)} %get-tuple-element.10.q_ref, f32[1536,512]{1,0:T(8,128)} %get-tuple-element.13.acc_in_ref, f32[1536,128]{1,0:T(8,128)} %get-tuple-element.14.ml_in_ref, bf16[1024,512]{1,0:T(8,128)(2,1)} %copy-done.5), custom_call_target="tpu_custom_call" | custom-call | flops 3221225472 | bytes 12582912 | tf_op jit(solution)/shard_map/prefix_last/pallas_call | solution.py:261
  (60 shorter events, 16.4 us)
Async XLA Ops:
  1.4 5.7 %collective-permute-start.2 = (bf16[128,4096]{1,0:T(8,128)(2,1)S(1)}, bf16[128,4096]{1,0:T(8,128)(2,1)}, u32[]{:S(2)}, u32[]{:S(2)}) collective-permute-start(bf16[128,4096]{1,0:T(8,128)(2,1)S(1)} %dynamic-slice_bitcast_fusion), channel_id=1, source_target_pairs={{0,8},{8,0},{16,24},{24,16},{32,40},{40,32},{48,56},{56,48},{64,72... | collective-permute-start | bytes 3145736 | tf_op jit(solution)/shard_map/ppermute | solution.py:28
  8.6 14.9 %collective-permute-start.3 = (bf16[64,4096]{1,0:T(8,128)(2,1)S(1)}, bf16[64,4096]{1,0:T(8,128)(2,1)S(1)}, u32[]{:S(2)}, u32[]{:S(2)}) collective-permute-start(bf16[64,4096]{1,0:T(8,128)(2,1)S(1)} %dynamic-slice_bitcast_fusion.1), channel_id=1, source_target_pairs={{0,128},{8,136},{16,144},{24,152},{32,160},{40,168},{48,176},{56,1... | collective-permute-start | bytes 1572872 | tf_op jit(solution)/shard_map/ppermute | solution.py:28
  9.9 19.0 %copy-start.3 = (f32[128]{0:T(128)S(1)}, f32[128]{0:T(128)}, u32[]{:S(2)}) copy-start(f32[128]{0:T(128)} %param.12) | copy-start | bytes 1540
  9.9 19.0 %copy-start.4 = (f32[128]{0:T(128)S(1)}, f32[128]{0:T(128)}, u32[]{:S(2)}) copy-start(f32[128]{0:T(128)} %param.11) | copy-start | bytes 1540
  9.9 20.8 %copy-start.1 = (bf16[1536,256]{1,0:T(8,128)(2,1)S(1)}, bf16[1536,256]{1,0:T(8,128)(2,1)}, u32[]{:S(2)}) copy-start(bf16[1536,256]{1,0:T(8,128)(2,1)} %k_ref.1) | copy-start | bytes 2359300
  23.6 12.1 %collective-permute-start.10 = (bf16[8,4096]{1,0:T(8,128)(2,1)S(1)}, bf16[8,4096]{1,0:T(8,128)(2,1)S(1)}, u32[]{:S(2)}, u32[]{:S(2)}) collective-permute-start(bf16[8,4096]{1,0:T(8,128)(2,1)S(1)} %get-tuple-element.15), channel_id=1, source_target_pairs={{0,64},{8,72},{16,80},{24,88},{32,96},{40,104},{48,112},{56,120},{... | collective-permute-start | bytes 196616 | tf_op jit(solution)/shard_map/ppermute | solution.py:28
  28.8 9.7 %collective-permute-start.4 = (bf16[8,4096]{1,0:T(8,128)(2,1)S(1)}, bf16[8,4096]{1,0:T(8,128)(2,1)S(1)}, u32[]{:S(2)}, u32[]{:S(2)}) collective-permute-start(bf16[8,4096]{1,0:T(8,128)(2,1)S(1)} %get-tuple-element.21), channel_id=1, source_target_pairs={{0,112},{8,120},{16,0},{24,8},{32,16},{40,24},{48,32},{56,40},{64,... | collective-permute-start | bytes 196616 | tf_op jit(solution)/shard_map/ppermute | solution.py:28
  31.7 8.7 %collective-permute-start.5 = (bf16[8,4096]{1,0:T(8,128)(2,1)S(1)}, bf16[8,4096]{1,0:T(8,128)(2,1)S(1)}, u32[]{:S(2)}, u32[]{:S(2)}) collective-permute-start(bf16[8,4096]{1,0:T(8,128)(2,1)S(1)} %get-tuple-element.20), channel_id=1, source_target_pairs={{0,16},{8,24},{16,32},{24,40},{32,48},{40,56},{48,64},{56,72},{64,... | collective-permute-start | bytes 196616 | tf_op jit(solution)/shard_map/ppermute | solution.py:28
  33.3 12.4 %collective-permute-start.6 = (bf16[8,4096]{1,0:T(8,128)(2,1)S(1)}, bf16[8,4096]{1,0:T(8,128)(2,1)S(1)}, u32[]{:S(2)}, u32[]{:S(2)}) collective-permute-start(bf16[8,4096]{1,0:T(8,128)(2,1)S(1)} %get-tuple-element.19), channel_id=1, source_target_pairs={{0,96},{8,104},{16,112},{24,120},{32,0},{40,8},{48,16},{56,24},{64... | collective-permute-start | bytes 196616 | tf_op jit(solution)/shard_map/ppermute | solution.py:28
  33.3 14.3 %collective-permute-start.7 = (bf16[8,4096]{1,0:T(8,128)(2,1)S(1)}, bf16[8,4096]{1,0:T(8,128)(2,1)S(1)}, u32[]{:S(2)}, u32[]{:S(2)}) collective-permute-start(bf16[8,4096]{1,0:T(8,128)(2,1)S(1)} %get-tuple-element.18), channel_id=1, source_target_pairs={{0,32},{8,40},{16,48},{24,56},{32,64},{40,72},{48,80},{56,88},{64,... | collective-permute-start | bytes 196616 | tf_op jit(solution)/shard_map/ppermute | solution.py:28
  35.6 12.0 %collective-permute-start.8 = (bf16[8,4096]{1,0:T(8,128)(2,1)S(1)}, bf16[8,4096]{1,0:T(8,128)(2,1)S(1)}, u32[]{:S(2)}, u32[]{:S(2)}) collective-permute-start(bf16[8,4096]{1,0:T(8,128)(2,1)S(1)} %get-tuple-element.17), channel_id=1, source_target_pairs={{0,80},{8,88},{16,96},{24,104},{32,112},{40,120},{48,0},{56,8},{64... | collective-permute-start | bytes 196616 | tf_op jit(solution)/shard_map/ppermute | solution.py:28
  38.5 9.1 %collective-permute-start.9 = (bf16[8,4096]{1,0:T(8,128)(2,1)S(1)}, bf16[8,4096]{1,0:T(8,128)(2,1)S(1)}, u32[]{:S(2)}, u32[]{:S(2)}) collective-permute-start(bf16[8,4096]{1,0:T(8,128)(2,1)S(1)} %get-tuple-element.16), channel_id=1, source_target_pairs={{0,48},{8,56},{16,64},{24,72},{32,80},{40,88},{48,96},{56,104},{64... | collective-permute-start | bytes 196616 | tf_op jit(solution)/shard_map/ppermute | solution.py:28
  40.5 56.8 %collective-permute-start = (bf16[1024,256]{1,0:T(8,128)(2,1)S(1)}, bf16[1024,256]{1,0:T(8,128)(2,1)S(1)}, u32[]{:S(2)}, u32[]{:S(2)}) collective-permute-start(bf16[1024,256]{1,0:T(8,128)(2,1)S(1)} %slice.9), channel_id=1, source_target_pairs={{0,8},{8,16},{16,24},{24,32},{32,40},{40,48},{48,56},{56,64},{64,7... | collective-permute-start | bytes 1572872 | tf_op jit(solution)/shard_map/ppermute | solution.py:277
  45.7 51.6 %collective-permute-start.1 = (bf16[1024,256]{1,0:T(8,128)(2,1)S(1)}, bf16[1024,256]{1,0:T(8,128)(2,1)S(1)}, u32[]{:S(2)}, u32[]{:S(2)}) collective-permute-start(bf16[1024,256]{1,0:T(8,128)(2,1)S(1)} %slice.10), channel_id=1, source_target_pairs={{0,8},{8,16},{16,24},{24,32},{32,40},{40,48},{48,56},{56,64},{64,7... | collective-permute-start | bytes 1572872 | tf_op jit(solution)/shard_map/ppermute | solution.py:278
  48.3 10.6 %all-to-all-start = ((bf16[8,8,512]{2,0,1:T(8,128)(2,1)}), bf16[8,8,512]{2,0,1:T(8,128)(2,1)S(1)}, u32[]{:S(2)}, u32[]{:S(2)}) async-start(bf16[8,8,512]{2,0,1:T(8,128)(2,1)} %bitcast.20), calls=%async_computation | async-start | bytes 131072 | tf_op jit(solution)/shard_map/all_to_all | solution.py:282
  58.9 7.2 %collective-permute-start.11 = (bf16[64,512]{1,0:T(8,128)(2,1)S(1)}, bf16[64,512]{1,0:T(8,128)(2,1)S(1)}, u32[]{:S(2)}, u32[]{:S(2)}) collective-permute-start(bf16[64,512]{1,0:T(8,128)(2,1)S(1)} %bitcast.63), channel_id=1, source_target_pairs={{0,64},{8,72},{16,80},{24,88},{32,96},{40,104},{48,112},{56,120},{... | collective-permute-start | bytes 196616 | tf_op jit(solution)/shard_map/ppermute | solution.py:28
  61.6 8.2 %collective-permute-start.12 = (bf16[64,512]{1,0:T(8,128)(2,1)S(1)}, bf16[64,512]{1,0:T(8,128)(2,1)S(1)}, u32[]{:S(2)}, u32[]{:S(2)}) collective-permute-start(bf16[64,512]{1,0:T(8,128)(2,1)S(1)} %bitcast.64), channel_id=1, source_target_pairs={{0,48},{8,56},{16,64},{24,72},{32,80},{40,88},{48,96},{56,104},{64... | collective-permute-start | bytes 196616 | tf_op jit(solution)/shard_map/ppermute | solution.py:28
  64.5 8.2 %collective-permute-start.13 = (bf16[64,512]{1,0:T(8,128)(2,1)S(1)}, bf16[64,512]{1,0:T(8,128)(2,1)S(1)}, u32[]{:S(2)}, u32[]{:S(2)}) collective-permute-start(bf16[64,512]{1,0:T(8,128)(2,1)S(1)} %bitcast.65), channel_id=1, source_target_pairs={{0,80},{8,88},{16,96},{24,104},{32,112},{40,120},{48,0},{56,8},{64... | collective-permute-start | bytes 196616 | tf_op jit(solution)/shard_map/ppermute | solution.py:28
  66.1 7.2 %collective-permute-start.14 = (bf16[64,512]{1,0:T(8,128)(2,1)S(1)}, bf16[64,512]{1,0:T(8,128)(2,1)S(1)}, u32[]{:S(2)}, u32[]{:S(2)}) collective-permute-start(bf16[64,512]{1,0:T(8,128)(2,1)S(1)} %bitcast.66), channel_id=1, source_target_pairs={{0,32},{8,40},{16,48},{24,56},{32,64},{40,72},{48,80},{56,88},{64,... | collective-permute-start | bytes 196616 | tf_op jit(solution)/shard_map/ppermute | solution.py:28
  69.8 7.9 %collective-permute-start.15 = (bf16[64,512]{1,0:T(8,128)(2,1)S(1)}, bf16[64,512]{1,0:T(8,128)(2,1)S(1)}, u32[]{:S(2)}, u32[]{:S(2)}) collective-permute-start(bf16[64,512]{1,0:T(8,128)(2,1)S(1)} %bitcast.67), channel_id=1, source_target_pairs={{0,96},{8,104},{16,112},{24,120},{32,0},{40,8},{48,16},{56,24},{64... | collective-permute-start | bytes 196616 | tf_op jit(solution)/shard_map/ppermute | solution.py:28
  72.7 5.1 %collective-permute-start.16 = (bf16[64,512]{1,0:T(8,128)(2,1)S(1)}, bf16[64,512]{1,0:T(8,128)(2,1)S(1)}, u32[]{:S(2)}, u32[]{:S(2)}) collective-permute-start(bf16[64,512]{1,0:T(8,128)(2,1)S(1)} %bitcast.68), channel_id=1, source_target_pairs={{0,16},{8,24},{16,32},{24,40},{32,48},{40,56},{48,64},{56,72},{64,... | collective-permute-start | bytes 196616 | tf_op jit(solution)/shard_map/ppermute | solution.py:28
  73.3 5.5 %collective-permute-start.17 = (bf16[64,512]{1,0:T(8,128)(2,1)S(1)}, bf16[64,512]{1,0:T(8,128)(2,1)S(1)}, u32[]{:S(2)}, u32[]{:S(2)}) collective-permute-start(bf16[64,512]{1,0:T(8,128)(2,1)S(1)} %bitcast.69), channel_id=1, source_target_pairs={{0,112},{8,120},{16,0},{24,8},{32,16},{40,24},{48,32},{56,40},{64,... | collective-permute-start | bytes 196616 | tf_op jit(solution)/shard_map/ppermute | solution.py:28
  78.8 10.2 %collective-permute-start.18 = (bf16[512,512]{1,0:T(8,128)(2,1)S(1)}, bf16[512,512]{1,0:T(8,128)(2,1)S(1)}, u32[]{:S(2)}, u32[]{:S(2)}) collective-permute-start(bf16[512,512]{1,0:T(8,128)(2,1)S(1)} %get-tuple-element.22), channel_id=1, source_target_pairs={{0,128},{8,136},{16,144},{24,152},{32,160},{40,168},{48,176},{56,1... | collective-permute-start | bytes 1572872 | tf_op jit(solution)/shard_map/ppermute | solution.py:28
  89.0 54.9 %collective-permute-start.19 = (bf16[1024,512]{1,0:T(8,128)(2,1)S(1)}, bf16[1024,512]{1,0:T(8,128)(2,1)S(1)}, u32[]{:S(2)}, u32[]{:S(2)}) collective-permute-start(bf16[1024,512]{1,0:T(8,128)(2,1)S(1)} %constant_dynamic-update-slice_fusion.8.p_ref), channel_id=1, source_target_pairs={{0,8},{8,0},{16,24},{24,16},{32,40},{40,32},{48,56},{56,48},{64,72... | collective-permute-start | bytes 3145736 | tf_op jit(solution)/shard_map/ppermute | solution.py:28
  (5 other events, 18.3 us)

commit v2 on v0

v2 whole, which is shorter than its diff:
```python
import functools

import jax
import jax.numpy as jnp
from jax import lax
from jax.experimental import pallas as pl
from jax.experimental.pallas import tpu as pltpu
from jax.sharding import Mesh, PartitionSpec as P

HD = 128
WINDOW = 1024
QSCALAR = 168
YH, NZ, NC, NH = 2, 8, 2, 8
SEQ = ("yh", "z", "core")
BAND_TILE = 256
TILE = 512
CHUNK = 256
NEG = -1e30
BIG = 1e30
VMEM_LIMIT = 36 * 1024 * 1024


def swapped(array, axis):
    return lax.ppermute(array, axis, [(0, 1), (1, 0)])


def round_z(array, r):
    return lax.ppermute(array, "z", [(i, (i + r) % NZ) for i in range(NZ)])


def pick(array, at):
    return lax.dynamic_index_in_dim(array, at, 0, keepdims=False)


def halved(part, axis, root_at):
    at = lax.axis_index(axis)
    part = part.reshape(2, part.shape[0] // 2, part.shape[1])
    came = swapped(pick(part, 1 - at), axis)
    return jnp.where(root_at == at, pick(part, at), came)


def normed(rows, gain, cosine, sine):
    mean_sq = jnp.mean(rows * rows, axis=-1, keepdims=True)
    rows = rows * lax.rsqrt(mean_sq + 1e-06) * gain
    return rows * cosine + pltpu.roll(rows, HD // 2, 1) * sine


def dot_t(a, b):
    return lax.dot_general(a, b, (((1,), (1,)), ((), ())), preferred_element_type=jnp.float32)


def packed(parts):
    lane = lax.broadcasted_iota(jnp.int32, (parts[0].shape[0], HD), 1)
    out = jnp.zeros((parts[0].shape[0], HD), jnp.float32)
    for at, part in enumerate(parts):
        out = jnp.where(lane == at, part, out)
    return out


def rows_at(t, tile):
    return pl.ds(pl.multiple_of(t * tile, tile), tile)


def columns_of(h):
    return slice(h * HD, (h + 1) * HD)


def prep_kernel(q_ref, k_ref, qg_ref, kg_ref, cos_ref, sin_ref, qn_ref, kn_ref):
    local = q_ref.shape[0]

    def own(t, _):
        at = rows_at(t, BAND_TILE)
        cosine, sine = cos_ref[at, :], sin_ref[at, :]
        for c in range(k_ref.shape[1] // HD):
            rows = k_ref[at, columns_of(c)].astype(jnp.float32)
            kn_ref[at, columns_of(c)] = normed(rows, kg_ref[...], cosine, sine).astype(jnp.bfloat16)
        for h in range(q_ref.shape[1] // HD):
            rows = q_ref[at, columns_of(h)].astype(jnp.float32)
            rows = normed(rows, qg_ref[...], cosine, sine) * QSCALAR ** (-0.5)
            qn_ref[at, columns_of(h)] = rows.astype(jnp.bfloat16)
        return 0

    lax.fori_loop(0, local // BAND_TILE, own, 0)


def attend(state, query, key, value, keep_score=None, dead=None):
    score = dot_t(query, key)
    if keep_score is not None:
        score = jnp.where(keep_score, score, NEG)
    top = jnp.max(score, axis=1, keepdims=True)
    if dead is not None:
        top = jnp.where(dead, NEG, top)
    if state is not None:
        top = jnp.maximum(state[0], top)
    minus = top if dead is None else jnp.where(dead, BIG, top)
    weight = jnp.exp(score - minus).astype(jnp.bfloat16)
    out = jnp.dot(weight, value, preferred_element_type=jnp.float32)
    if state is not None:
        out = state[1] * jnp.exp(state[0] - top) + out
    return top, out


def band_kernel(
    first_ref, q_ref, before_ref, k_ref, v_ref, kg_ref, cos_ref, sin_ref,
    acc_ref, ml_ref, ke_ref, va_ref,
):
    local = q_ref.shape[0]
    kv = k_ref.shape[1] // HD
    group = q_ref.shape[1] // HD // kv
    for c in range(kv):
        va_ref[:WINDOW, columns_of(2 * c)] = before_ref[:, columns_of(kv + c)]
        va_ref[WINDOW:, columns_of(2 * c)] = v_ref[:, columns_of(c)]
        va_ref[:, columns_of(2 * c + 1)] = jnp.ones((WINDOW + local, HD), jnp.bfloat16)
    ke_ref[WINDOW:, :] = k_ref[...]

    def halo(t, _):
        at = rows_at(t, BAND_TILE)
        for c in range(kv):
            rows = before_ref[at, columns_of(c)].astype(jnp.float32)
            ke_ref[at, columns_of(c)] = normed(
                rows, kg_ref[...], cos_ref[at, :], sin_ref[at, :]
            ).astype(jnp.bfloat16)
        return 0

    lax.fori_loop(0, WINDOW // BAND_TILE, halo, 0)

    rows_in = lax.broadcasted_iota(jnp.int32, (group * BAND_TILE, CHUNK), 0) % BAND_TILE
    columns_in = lax.broadcasted_iota(jnp.int32, (group * BAND_TILE, CHUNK), 1)
    early = columns_in > rows_in
    late = columns_in <= rows_in
    before_blocks = WINDOW // CHUNK
    is_first = first_ref[0] == 1

    def band(t, _):
        at = rows_at(t, BAND_TILE)
        state = [None] * kv
        for j in range(before_blocks, -1, -1):
            keys_at = rows_at(t + j, CHUNK)
            for c in range(kv):
                query = jnp.concatenate(
                    [q_ref[at, columns_of(c * group + g)] for g in range(group)], axis=0
                )
                state[c] = attend(
                    state[c],
                    query,
                    ke_ref[keys_at, columns_of(c)],
                    va_ref[keys_at, 2 * c * HD : (2 * c + 2) * HD],
                    keep_score=late if j == before_blocks else early if j == 0 else None,
                    dead=None if j == before_blocks else is_first & (t + j < before_blocks),
                )
        tops, totals = [], []
        for c in range(kv):
            for g in range(group):
                mine = slice(g * BAND_TILE, (g + 1) * BAND_TILE)
                acc_ref[at, columns_of(c * group + g)] = state[c][1][mine, :HD]
                tops.append(state[c][0][mine])
                totals.append(state[c][1][mine, HD:])
        ml_ref[at, :] = packed(tops + totals)
        return 0

    lax.fori_loop(0, local // BAND_TILE, band, 0)


def prefix_kernel(last, pieces, q_ref, acc_in_ref, ml_in_ref, *rest):
    p_refs, rest = rest[:pieces], rest[pieces:]
    if last:
        out_ref, va_ref = rest
    else:
        acc_ref, ml_ref, va_ref = rest
    local = q_ref.shape[0]
    tokens = p_refs[0].shape[0]
    kv = p_refs[0].shape[1] // (2 * HD)
    group = q_ref.shape[1] // HD // kv
    for c in range(kv):
        for i, p_ref in enumerate(p_refs):
            va_ref[i * tokens : (i + 1) * tokens, columns_of(2 * c)] = p_ref[:, columns_of(2 * c + 1)]
        va_ref[:, columns_of(2 * c + 1)] = jnp.ones((pieces * tokens, HD), jnp.bfloat16)

    def step(t, _):
        at = rows_at(t, TILE)
        count = kv * group
        queries, state = [], []
        for c in range(kv):
            heads = range(c * group, (c + 1) * group)
            queries.append(jnp.concatenate([q_ref[at, columns_of(h)] for h in heads], axis=0))
            top = jnp.concatenate([ml_in_ref[at, h : h + 1] for h in heads], axis=0)
            total = jnp.concatenate([ml_in_ref[at, count + h : count + h + 1] for h in heads], axis=0)
            summed = jnp.concatenate([acc_in_ref[at, columns_of(h)] for h in heads], axis=0)
            both = jnp.concatenate([summed, jnp.broadcast_to(total, summed.shape)], axis=1)
            state.append((top, both))
        for i, p_ref in enumerate(p_refs):
            for j in range(tokens // CHUNK):
                at_keys = slice(j * CHUNK, (j + 1) * CHUNK)
                at_values = slice(i * tokens + j * CHUNK, i * tokens + (j + 1) * CHUNK)
                for c in range(kv):
                    state[c] = attend(
                        state[c],
                        queries[c],
                        p_ref[at_keys, columns_of(2 * c)],
                        va_ref[at_values, 2 * c * HD : (2 * c + 2) * HD],
                    )
        tops, totals = [], []
        for c in range(kv):
            top, both = state[c]
            if last:
                both = (both[:, :HD] / both[:, HD:]).astype(jnp.bfloat16)
            for g in range(group):
                mine = slice(g * TILE, (g + 1) * TILE)
                if last:
                    out_ref[at, columns_of(c * group + g)] = both[mine]
                else:
                    acc_ref[at, columns_of(c * group + g)] = both[mine, :HD]
                    tops.append(top[mine])
                    totals.append(both[mine, HD:])
        if not last:
            ml_ref[at, :] = packed(tops + totals)
        return 0

    lax.fori_loop(0, local // TILE, step, 0)


WHOLE = pl.BlockSpec(memory_space=pltpu.VMEM)
PARAMS = pltpu.CompilerParams(vmem_limit_bytes=VMEM_LIMIT)


def cost(pairs, in_out):
    return pl.CostEstimate(flops=8 * pairs * HD, transcendentals=pairs, bytes_accessed=in_out)


def prep(q, k, q_gain, k_gain, cosine, sine):
    return pl.pallas_call(
        prep_kernel,
        out_shape=(
            jax.ShapeDtypeStruct(q.shape, jnp.bfloat16),
            jax.ShapeDtypeStruct(k.shape, jnp.bfloat16),
        ),
        in_specs=[WHOLE] * 6,
        out_specs=(WHOLE,) * 2,
        compiler_params=PARAMS,
        cost_estimate=pl.CostEstimate(flops=40 * q.size, transcendentals=q.shape[0] * 6, bytes_accessed=8 << 20),
        name="prep",
    )(q, k, q_gain, k_gain, cosine, sine)


def band_part(first, q, before, k, v, k_gain, cosine, sine):
    local, width = q.shape
    return pl.pallas_call(
        band_kernel,
        out_shape=(
            jax.ShapeDtypeStruct((local, width), jnp.float32),
            jax.ShapeDtypeStruct((local, HD), jnp.float32),
        ),
        in_specs=[pl.BlockSpec(memory_space=pltpu.SMEM)] + [WHOLE] * 7,
        out_specs=(WHOLE,) * 2,
        scratch_shapes=[
            pltpu.VMEM((WINDOW + local, k.shape[1]), jnp.bfloat16),
            pltpu.VMEM((WINDOW + local, 2 * k.shape[1]), jnp.bfloat16),
        ],
        compiler_params=PARAMS,
        cost_estimate=cost(local * (width // HD) * (WINDOW + BAND_TILE), 10 << 20),
        name="band",
    )(first, q, before, k, v, k_gain, cosine, sine)


def prefix_part(last, q, acc, ml, *pieces):
    local, width = q.shape
    rows, columns = pieces[0].shape
    if last:
        out_shape = jax.ShapeDtypeStruct((local, width), jnp.bfloat16)
        out_specs = WHOLE
    else:
        out_shape = (
            jax.ShapeDtypeStruct((local, width), jnp.float32),
            jax.ShapeDtypeStruct((local, HD), jnp.float32),
        )
        out_specs = (WHOLE,) * 2
    return pl.pallas_call(
        functools.partial(prefix_kernel, last, len(pieces)),
        out_shape=out_shape,
        in_specs=[WHOLE] * (3 + len(pieces)),
        out_specs=out_specs,
        scratch_shapes=[pltpu.VMEM((len(pieces) * rows, columns), jnp.bfloat16)],
        compiler_params=PARAMS,
        cost_estimate=cost(local * (width // HD) * len(pieces) * rows, 10 << 20),
        name="prefix_last" if last else "prefix",
    )(q, acc, ml, *pieces)


def on_device(queries, keys, values, q_gain, k_gain, positions, prefix_cache, owner):
    local = queries.shape[0]
    root = owner[0]
    root_y, root_z, root_c = root // (NZ * NC), (root // NC) % NZ, root % NC

    slab = halved(prefix_cache[0], "core", root_c)
    onward = [(i, i + 1) for i in range(YH * NZ * NC - 1)]
    tail = jnp.concatenate([keys[local - WINDOW :], values[local - WINDOW :]], axis=1)
    slab, tail = lax.optimization_barrier((slab, tail))
    before = lax.ppermute(tail, SEQ, onward)
    slab = halved(slab, "yh", root_y)

    half = HD // 2
    freq = 10000.0 ** (-(jnp.arange(half).astype(jnp.float32) * 2.0) / HD)
    extended = positions[0] + jnp.arange(-WINDOW, local, dtype=jnp.int32)
    angle = extended.astype(jnp.float32)[:, None] * freq[None, :]
    cosine, sine = jnp.cos(angle), jnp.sin(angle)
    cosine = jnp.concatenate([cosine, cosine], axis=1)
    sine = jnp.concatenate([-sine, sine], axis=1)
    cosine, sine, slab = lax.optimization_barrier((cosine, sine, slab))

    rows, wide = slab.shape
    parts = slab.reshape(NZ, rows // NZ, NH, wide // NH).transpose(0, 2, 1, 3)
    parts = parts.reshape(NZ * NH, rows // NZ, wide // NH)
    parts = lax.all_to_all(parts, ("z", "head"), split_axis=0, concat_axis=0, tiled=True)
    query, key = prep(
        queries, keys, (1.0 + q_gain)[None], (1.0 + k_gain)[None], cosine[WINDOW:], sine[WINDOW:]
    )
    first = (lax.axis_index(SEQ) == 0).astype(jnp.int32).reshape(1)
    acc, ml = band_part(
        first, query, before, key, values, (1.0 + k_gain)[None], cosine[:WINDOW], sine[:WINDOW]
    )
    mine = pick(parts.reshape(NZ, NH, rows // NZ, wide // NH), root_z)
    mine = mine.reshape(NH * rows // NZ, wide // NH)
    mine, ml = lax.optimization_barrier((mine, ml))

    mine = jnp.concatenate([mine, round_z(mine, NZ // 2)], axis=0)
    mine = jnp.concatenate([mine, round_z(mine, 1), round_z(mine, -1), round_z(mine, 2)], axis=0)
    far = swapped(mine, "yh")
    acc, ml = prefix_part(False, query, acc, ml, mine, swapped(mine, "core"))
    far, ml = lax.optimization_barrier((far, ml))
    last = swapped(far, "core")
    acc, ml = prefix_part(False, query, acc, ml, far)
    return prefix_part(True, query, acc, ml, last)


def solution(mesh):
    fine = Mesh(mesh.devices.reshape(YH, NZ, NC, NH), SEQ + ("head",))
    return jax.shard_map(
        on_device,
        mesh=fine,
        in_specs=(
            P(SEQ, "head"),
            P(SEQ, "head"),
            P(SEQ, "head"),
            P(),
            P(),
            P(SEQ),
            P(SEQ, "head", None),
            P(),
        ),
        out_specs=P(SEQ, "head"),
        check_vma=False,
    )
```

time: 523 us -> 127 us (0.24)
  waiting for transfers between devices: 277 us -> 8.6 us
  matrix products: 71.1 us -> 0 us
  other arithmetic: 82.9 us -> 12.6 us
  Pallas kernels: 0 us -> 54.3 us
  local copies, waits for them, and re-layouts: 64.3 us -> 13 us
  starting transfers between devices: 9.58 us -> 37.4 us
  between operations: 14.2 us -> 1.02 us
    psum x1 -> x0, waiting for transfers between devices: 256 us -> none  [spread(): return lax.psum(jnp.where(mine, array, jnp.zeros_like(array)), axis)]
    dot_general x12 -> x0, matrix products: 71.1 us -> none  [the longest x3 28.5 us: one_block(): jnp.einsum('kgit,tkd->kgid', exp_pre.astype(jnp.bfloat16), prefix_value,...]
    pallas_call x0 -> x5, Pallas kernels: none -> 54.3 us  [the longest x3 34.8 us: prefix_part(): pl.pallas_call(functools.partial(prefix_kernel, last, len(pieces)), out_s...]
    reduce_sum x8 -> x0, other arithmetic: 34.1 us -> none  [the longest x6 31.1 us: one_block(): total = jnp.sum(exp_band, axis=-1) + jnp.sum(exp_pre, axis=-1)]
    unnamed x19 -> x25, local copies, waits for them, and re-layouts: 30.5 us -> 6.03 us
    unnamed x1 -> x0, other arithmetic: 22.9 us -> none
    all_to_all x1, waiting for transfers between devices: 21.1 us -> 0.01 us  [on_device(): lax.all_to_all(parts, ('z', 'head'), split_axis=0, concat_axis=0, tiled=T...]
    ppermute x1 -> x10, starting transfers between devices: 5.24 us -> 26.3 us  [the longest x5 11.5 us: swapped(): return lax.ppermute(array, axis, [(0, 1), (1, 0)])]
  transfers between devices with their start and end apart: 3 -> 11, of which waited for: 2 -> 3; matrix products, arithmetic and copies ran while one was open for 11% -> 13% of each run, Pallas kernels for 0% -> 35%
where the time goes in v2:
time: 127 us
  Pallas kernels  54.3 us (43%)
  starting transfers between devices  37.4 us (29%)
  local copies, waits for them, and re-layouts  13 us (10%)
  other arithmetic  12.6 us (10%)
  waiting for transfers between devices  8.6 us (7%)
    pallas_call x3, Pallas kernels, prefix_part(): pl.pallas_call(functools.partial(prefix_kernel, last, len(pieces)), out_s...  34.8 us
    pallas_call x1, Pallas kernels, band_part(): pl.pallas_call(band_kernel, out_shape=(jax.ShapeDtypeStruct((local, width...  14.3 us
    ppermute x5, starting transfers between devices, swapped(): return lax.ppermute(array, axis, [(0, 1), (1, 0)])  11.5 us
    all_to_all x1, starting transfers between devices, on_device(): lax.all_to_all(parts, ('z', 'head'), split_axis=0, concat_axis=0, tiled=T...  11.1 us
    ppermute x4, starting transfers between devices, round_z(): return lax.ppermute(array, 'z', [(i, (i + r) % NZ) for i in range(NZ)])  9.61 us
    ppermute x4, waiting for transfers between devices, round_z(): return lax.ppermute(array, 'z', [(i, (i + r) % NZ) for i in range(NZ)])  8.58 us
    unnamed x25, local copies, waits for them, and re-layouts  6.03 us
    neg x1, other arithmetic, on_device(): sine = jnp.concatenate([-sine, sine], axis=1)  5.99 us
  transfers between devices with their start and end apart: 11, of which 3 were waited for; matrix products, arithmetic and copies ran while one was open for 13% of the time, Pallas kernels for 35%

profile of v2, /device:TPU:1, one launch (start us, length us, event | category | flops | bytes accessed | tf_op | source)
XLA Modules:
  0.0 127.0 jit_solution(1844709021805500875)
XLA Ops:
  0.0 2.3 %dynamic-slice_bitcast_fusion = bf16[128,4096]{1,0:T(8,128)(2,1)} fusion(bf16[2,128,4096]{2,1,0:T(8,128)(2,1)} %bitcast.31, s32[]{:T(128)S(6)} %select_n.57), kind=kLoop, calls=%fused_computation.6 | loop fusion | bytes 2097156 | tf_op jit(solution)/shard_map/jit(dynamic_index_in_dim)/squeeze | solution.py:32
  2.3 3.2 %collective-permute-start = (bf16[128,4096]{1,0:T(8,128)(2,1)}, bf16[128,4096]{1,0:T(8,128)(2,1)}, u32[]{:S(2)}, u32[]{:S(2)}) collective-permute-start(bf16[128,4096]{1,0:T(8,128)(2,1)} %dynamic-slice_bitcast_fusion), channel_id=1, source_target_pairs={{0,8},{8,0},{1,9},{9,1},{2,10},{10,2},{3,11},{11,3},{4,12},{12,4},... | collective-permute-start | bytes 3145736 | tf_op jit(solution)/shard_map/ppermute | solution.py:24
  6.2 1.3 %slice.21 = s32[1]{0:T(128)} slice(s32[1536]{0:T(1024)} %param.13), slice={[0:1]} | slice | bytes 8 | tf_op jit(solution)/shard_map/slice | solution.py:303
  10.3 1.2 collective-permute-start.1
  11.5 6.0 %fusion = (f32[2560,64]{1,0:T(8,128)S(1)}, f32[2560,64]{1,0:T(8,128)S(1)}, f32[2560,64]{1,0:T(8,128)}) fusion(f32[64]{0:T(128)S(1)} %multiply_power_fusion, f32[2560]{0:T(1024)S(1)} %add_convert_fusion), kind=kLoop, calls=%fused_computation.9 | loop fusion | flops 327680 | bytes 1976576 | tf_op jit(solution)/shard_map/neg | solution.py:307
  17.5 4.0 %pad_maximum_fusion = (f32[2560,128]{1,0:T(8,128)}, f32[2560,128]{1,0:T(8,128)}) fusion(f32[2560,64]{1,0:T(8,128)} %get-tuple-element.45, f32[2560,64]{1,0:T(8,128)S(1)} %get-tuple-element.44, f32[2560,64]{1,0:T(8,128)S(1)} %get-tuple-element.43), kind=kLoop, calls=%fused_computation.2 | loop fusion | flops 655360 | bytes 4587520 | tf_op jit(solution)/shard_map/concatenate | solution.py:306
  21.5 5.1 %collective-permute-start.2 = (bf16[1024,512]{1,0:T(8,128)(2,1)}, bf16[1024,512]{1,0:T(8,128)(2,1)S(1)}, u32[]{:S(2)}, u32[]{:S(2)}) collective-permute-start(bf16[1024,512]{1,0:T(8,128)(2,1)} %pad_maximum_fusion.2), channel_id=1, source_target_pairs={{0,8},{8,16},{16,24},{24,32},{32,40},{40,48},{48,56},{56,64},{64,7... | collective-permute-start | bytes 3145736 | tf_op jit(solution)/shard_map/ppermute | solution.py:298
  27.5 11.1 %all-to-all-start = ((bf16[64,8,512]{2,1,0:T(8,128)(2,1)}), bf16[64,8,512]{2,1,0:T(8,128)(2,1)}, u32[]{:S(2)}, u32[]{:S(2)}) async-start(bf16[64,8,512]{2,1,0:T(8,128)(2,1)} %bitcast.13), calls=%async_computation | async-start | bytes 1048576 | tf_op jit(solution)/shard_map/all_to_all | solution.py:313
  38.8 1.3 %slice.24.cos_ref = f32[1536,128]{1,0:T(8,128)S(1)} slice(f32[2560,128]{1,0:T(8,128)} %get-tuple-element.23), slice={[1024:2560], [0:128]} | slice | bytes 1572864 | tf_op jit(solution)/shard_map/slice | solution.py:315
  42.8 5.2 %prep.1 = (bf16[1536,512]{1,0:T(8,128)(2,1)S(1)}, bf16[1536,256]{1,0:T(8,128)(2,1)S(1)}) custom-call(bf16[1536,512]{1,0:T(8,128)(2,1)S(1)} %copy-done.1, bf16[1536,256]{1,0:T(8,128)(2,1)S(1)} %copy-done, f32[1,128]{1,0:T(1,128)S(1)} %add_bitcast_fusion.1.qg_ref, f32[1,128]{1,0:T(1,128)S(1)} %add_bitcast_fusion.kg_ref, f32[1536,128]{1,0:T(8,128)S(1)} %slice.24.cos_ref, ...), custom_call_target="tpu_custom_call" | custom-call | flops 31457280 | bytes 8388608 | tf_op jit(solution)/shard_map/prep/pallas_call | solution.py:231
  48.1 14.3 %band.1 = (f32[1536,512]{1,0:T(8,128)S(1)}, f32[1536,128]{1,0:T(8,128)S(1)}) custom-call(s32[1]{0:T(128)} %bitcast.10.first_ref, bf16[1536,512]{1,0:T(8,128)(2,1)S(1)} %get-tuple-element.25.q_ref, bf16[1024,512]{1,0:T(8,128)(2,1)S(1)} %collective-permute-done.2.before_ref, bf16[1536,256]{1,0:T(8,128)(2,1)S(1)} %get-tuple-element.27.k_ref, ...), custom_call_target="tpu_custom_call" | custom-call | flops 8053063680 | bytes 10485760 | tf_op jit(solution)/shard_map/band/pallas_call | solution.py:247
  62.4 1.6 %copy-done.3 = f32[1536,512]{1,0:T(8,128)} copy-done((f32[1536,512]{1,0:T(8,128)}, f32[1536,512]{1,0:T(8,128)S(1)}, u32[]{:S(2)}) %copy-start.3) | copy-done | bytes 3145752
  64.9 5.0 %collective-permute-start.3 = (bf16[64,512]{1,0:T(8,128)(2,1)S(1)}, bf16[64,512]{1,0:T(8,128)(2,1)S(1)}, u32[]{:S(2)}, u32[]{:S(2)}) collective-permute-start(bf16[64,512]{1,0:T(8,128)(2,1)S(1)} %dynamic-slice_bitcast_fusion.2), channel_id=1, source_target_pairs={{0,64},{16,80},{32,96},{48,112},{64,0},{80,16},{96,32},{112,48},{1... | collective-permute-start | bytes 196616 | tf_op jit(solution)/shard_map/ppermute | solution.py:28
  69.9 2.2 %collective-permute-done.3 = bf16[64,512]{1,0:T(8,128)(2,1)S(1)} collective-permute-done((bf16[64,512]{1,0:T(8,128)(2,1)S(1)}, bf16[64,512]{1,0:T(8,128)(2,1)S(1)}, u32[]{:S(2)}, u32[]{:S(2)}) %collective-permute-start.3) | collective-permute-done | bytes 65568 | tf_op jit(solution)/shard_map/ppermute | solution.py:28
  72.1 1.3 %collective-permute-start.4 = (bf16[128,512]{1,0:T(8,128)(2,1)S(1)}, bf16[128,512]{1,0:T(8,128)(2,1)S(1)}, u32[]{:S(2)}, u32[]{:S(2)}) collective-permute-start(bf16[128,512]{1,0:T(8,128)(2,1)S(1)} %get-tuple-element.39), channel_id=1, source_target_pairs={{0,16},{16,32},{32,48},{48,64},{64,80},{80,96},{96,112},{112,0},{1... | collective-permute-start | bytes 393224 | tf_op jit(solution)/shard_map/ppermute | solution.py:28
  73.4 3.0 %collective-permute-start.5 = (bf16[128,512]{1,0:T(8,128)(2,1)S(1)}, bf16[128,512]{1,0:T(8,128)(2,1)S(1)}, u32[]{:S(2)}, u32[]{:S(2)}) collective-permute-start(bf16[128,512]{1,0:T(8,128)(2,1)S(1)} %get-tuple-element.39), channel_id=1, source_target_pairs={{0,112},{16,0},{32,16},{48,32},{64,48},{80,64},{96,80},{112,96},{1... | collective-permute-start | bytes 393224 | tf_op jit(solution)/shard_map/ppermute | solution.py:28
  76.7 1.9 %collective-permute-done.4 = bf16[128,512]{1,0:T(8,128)(2,1)S(1)} collective-permute-done((bf16[128,512]{1,0:T(8,128)(2,1)S(1)}, bf16[128,512]{1,0:T(8,128)(2,1)S(1)}, u32[]{:S(2)}, u32[]{:S(2)}) %collective-permute-start.4) | collective-permute-done | bytes 131104 | tf_op jit(solution)/shard_map/ppermute | solution.py:28
  78.7 4.5 %collective-permute-done.6 = bf16[128,512]{1,0:T(8,128)(2,1)S(1)} collective-permute-done((bf16[128,512]{1,0:T(8,128)(2,1)S(1)}, bf16[128,512]{1,0:T(8,128)(2,1)S(1)}, u32[]{:S(2)}, u32[]{:S(2)}) %collective-permute-start.6) | collective-permute-done | bytes 131104 | tf_op jit(solution)/shard_map/ppermute | solution.py:28
  83.2 4.2 %collective-permute-start.7 = (bf16[512,512]{1,0:T(8,128)(2,1)S(1)}, bf16[512,512]{1,0:T(8,128)(2,1)S(1)}, u32[]{:S(2)}, u32[]{:S(2)}) collective-permute-start(bf16[512,512]{1,0:T(8,128)(2,1)S(1)} %constant_dynamic-update-slice_fusion.2.rest_0_), channel_id=1, source_target_pairs={{0,8},{8,0},{1,9},{9,1},{2,10},{10,2},{3,11},{11,3},{4,12},{12,4},... | collective-permute-start | bytes 1572872 | tf_op jit(solution)/shard_map/ppermute | solution.py:24
  87.3 2.3 %collective-permute-start.8 = (bf16[512,512]{1,0:T(8,128)(2,1)S(1)}, bf16[512,512]{1,0:T(8,128)(2,1)S(1)}, u32[]{:S(2)}, u32[]{:S(2)}) collective-permute-start(bf16[512,512]{1,0:T(8,128)(2,1)S(1)} %constant_dynamic-update-slice_fusion.2.rest_0_), channel_id=1, source_target_pairs={{0,128},{128,0},{1,129},{129,1},{2,130},{130,2},{3,131},{131,3},{4... | collective-permute-start | bytes 1572872 | tf_op jit(solution)/shard_map/ppermute | solution.py:24
  89.7 1.9 %copy-done.4 = f32[1536,512]{1,0:T(8,128)S(1)} copy-done((f32[1536,512]{1,0:T(8,128)S(1)}, f32[1536,512]{1,0:T(8,128)}, u32[]{:S(2)}) %copy-start.4) | copy-done | bytes 3145752
  91.6 15.7 %prefix.2 = (f32[1536,512]{1,0:T(8,128)S(1)}, f32[1536,128]{1,0:T(8,128)S(1)}) custom-call(bf16[1536,512]{1,0:T(8,128)(2,1)S(1)} %get-tuple-element.25.q_ref, f32[1536,512]{1,0:T(8,128)S(1)} %copy-done.4, f32[1536,128]{1,0:T(8,128)S(1)} %get-tuple-element.31.ml_in_ref, bf16[512,512]{1,0:T(8,128)(2,1)S(1)} %constant_dynamic-update-slice_fusion.2.rest_0_, ...), custom_call_target="tpu_custom_call" | custom-call | flops 6442450944 | bytes 10485760 | tf_op jit(solution)/shard_map/prefix/pallas_call | solution.py:277
  107.9 9.1 %prefix.3 = (f32[1536,512]{1,0:T(8,128)S(1)}, f32[1536,128]{1,0:T(8,128)S(1)}) custom-call(bf16[1536,512]{1,0:T(8,128)(2,1)S(1)} %get-tuple-element.25.q_ref, f32[1536,512]{1,0:T(8,128)S(1)} %get-tuple-element.33.acc_in_ref, f32[1536,128]{1,0:T(8,128)S(1)} %get-tuple-element.35.ml_in_ref, bf16[512,512]{1,0:T(8,128)(2,1)S(1)} %collective-permute-done.8.rest_0_), custom_call_target="tpu_custom_call" | custom-call | flops 3221225472 | bytes 10485760 | tf_op jit(solution)/shard_map/prefix/pallas_call | solution.py:277
  117.1 10.0 %prefix_last.1 = bf16[1536,512]{1,0:T(8,128)(2,1)} custom-call(bf16[1536,512]{1,0:T(8,128)(2,1)S(1)} %get-tuple-element.25.q_ref, f32[1536,512]{1,0:T(8,128)S(1)} %get-tuple-element.37.acc_in_ref, f32[1536,128]{1,0:T(8,128)S(1)} %get-tuple-element.38.ml_in_ref, bf16[512,512]{1,0:T(8,128)(2,1)S(1)} %collective-permute-done.9.rest_0_), custom_call_target="tpu_custom_call" | custom-call | flops 3221225472 | bytes 10485760 | tf_op jit(solution)/shard_map/prefix_last/pallas_call | solution.py:277
  (51 shorter events, 8.2 us)
Async XLA Ops:
  2.3 5.8 %slice-start = ((bf16[1536,256]{1,0:T(8,128)(2,1)}), bf16[1024,256]{1,0:T(8,128)(2,1)S(1)}, s32[]{:S(2)}) async-start(bf16[1536,256]{1,0:T(8,128)(2,1)} %k_ref.1), calls=%async_computation.1 | async-start | bytes 1048576 | tf_op jit(solution)/shard_map/slice | solution.py:296
  2.3 5.8 %slice-start.1 = ((bf16[1536,256]{1,0:T(8,128)(2,1)}), bf16[1024,256]{1,0:T(8,128)(2,1)S(1)}, s32[]{:S(2)}) async-start(bf16[1536,256]{1,0:T(8,128)(2,1)} %v_ref.1), calls=%async_computation.2 | async-start | bytes 1048576 | tf_op jit(solution)/shard_map/slice | solution.py:296
  2.3 6.9 %collective-permute-start = (bf16[128,4096]{1,0:T(8,128)(2,1)}, bf16[128,4096]{1,0:T(8,128)(2,1)}, u32[]{:S(2)}, u32[]{:S(2)}) collective-permute-start(bf16[128,4096]{1,0:T(8,128)(2,1)} %dynamic-slice_bitcast_fusion), channel_id=1, source_target_pairs={{0,8},{8,0},{1,9},{9,1},{2,10},{10,2},{3,11},{11,3},{4,12},{12,4},... | collective-permute-start | bytes 3145736 | tf_op jit(solution)/shard_map/ppermute | solution.py:24
  6.2 3.0 %copy-start.8 = (bf16[1,256,4096]{2,1,0:T(8,128)(2,1)S(1)}, bf16[1,256,4096]{2,1,0:T(8,128)(2,1)}, u32[]{:S(2)}) copy-start(bf16[1,256,4096]{2,1,0:T(8,128)(2,1)} %param.14) | copy-start | bytes 6291460
  9.3 1.0 copy-start.6
  10.3 16.4 %collective-permute-start.1 = (bf16[64,4096]{1,0:T(8,128)(2,1)S(1)}, bf16[64,4096]{1,0:T(8,128)(2,1)}, u32[]{:S(2)}, u32[]{:S(2)}) collective-permute-start(bf16[64,4096]{1,0:T(8,128)(2,1)S(1)} %dynamic-slice_bitcast_fusion.1), channel_id=1, source_target_pairs={{0,128},{128,0},{1,129},{129,1},{2,130},{130,2},{3,131},{131,3},{4... | collective-permute-start | bytes 1572872 | tf_op jit(solution)/shard_map/ppermute | solution.py:24
  17.5 9.2 %copy-start.7 = (bf16[128,4096]{1,0:T(8,128)(2,1)S(1)}, bf16[128,4096]{1,0:T(8,128)(2,1)}, u32[]{:S(2)}) copy-start(bf16[128,4096]{1,0:T(8,128)(2,1)} %copy-done.6) | copy-start | bytes 3145732
  21.5 17.2 %copy-start.9 = (f32[128]{0:T(128)S(1)}, f32[128]{0:T(128)}, u32[]{:S(2)}) copy-start(f32[128]{0:T(128)} %param.12) | copy-start | bytes 1540
  21.5 17.3 %copy-start.10 = (f32[128]{0:T(128)S(1)}, f32[128]{0:T(128)}, u32[]{:S(2)}) copy-start(f32[128]{0:T(128)} %param.11) | copy-start | bytes 1540
  21.5 26.6 %collective-permute-start.2 = (bf16[1024,512]{1,0:T(8,128)(2,1)}, bf16[1024,512]{1,0:T(8,128)(2,1)S(1)}, u32[]{:S(2)}, u32[]{:S(2)}) collective-permute-start(bf16[1024,512]{1,0:T(8,128)(2,1)} %pad_maximum_fusion.2), channel_id=1, source_target_pairs={{0,8},{8,16},{16,24},{24,32},{32,40},{40,48},{48,56},{56,64},{64,7... | collective-permute-start | bytes 3145736 | tf_op jit(solution)/shard_map/ppermute | solution.py:298
  27.5 36.5 %all-to-all-start = ((bf16[64,8,512]{2,1,0:T(8,128)(2,1)}), bf16[64,8,512]{2,1,0:T(8,128)(2,1)}, u32[]{:S(2)}, u32[]{:S(2)}) async-start(bf16[64,8,512]{2,1,0:T(8,128)(2,1)} %bitcast.13), calls=%async_computation | async-start | bytes 1048576 | tf_op jit(solution)/shard_map/all_to_all | solution.py:313
  38.8 2.4 %copy-start.5 = (f32[2560,128]{1,0:T(8,128)S(1)}, f32[2560,128]{1,0:T(8,128)}, u32[]{:S(2)}) copy-start(f32[2560,128]{1,0:T(8,128)} %get-tuple-element.24) | copy-start | bytes 3932164
  41.2 1.1 copy-start
  41.2 1.6 %copy-start.1 = (bf16[1536,512]{1,0:T(8,128)(2,1)S(1)}, bf16[1536,512]{1,0:T(8,128)(2,1)}, u32[]{:S(2)}) copy-start(bf16[1536,512]{1,0:T(8,128)(2,1)} %q_ref.1) | copy-start | bytes 4718596
  42.8 5.3 %copy-start.2 = (bf16[1536,256]{1,0:T(8,128)(2,1)S(1)}, bf16[1536,256]{1,0:T(8,128)(2,1)}, u32[]{:S(2)}) copy-start(bf16[1536,256]{1,0:T(8,128)(2,1)} %v_ref.1) | copy-start | bytes 2359300
  62.4 1.6 %copy-start.3 = (f32[1536,512]{1,0:T(8,128)}, f32[1536,512]{1,0:T(8,128)S(1)}, u32[]{:S(2)}) copy-start(f32[1536,512]{1,0:T(8,128)S(1)} %get-tuple-element.28.acc_in_ref) | copy-start | bytes 9437188
  64.9 7.1 %collective-permute-start.3 = (bf16[64,512]{1,0:T(8,128)(2,1)S(1)}, bf16[64,512]{1,0:T(8,128)(2,1)S(1)}, u32[]{:S(2)}, u32[]{:S(2)}) collective-permute-start(bf16[64,512]{1,0:T(8,128)(2,1)S(1)} %dynamic-slice_bitcast_fusion.2), channel_id=1, source_target_pairs={{0,64},{16,80},{32,96},{48,112},{64,0},{80,16},{96,32},{112,48},{1... | collective-permute-start | bytes 196616 | tf_op jit(solution)/shard_map/ppermute | solution.py:28
  72.1 6.6 %collective-permute-start.4 = (bf16[128,512]{1,0:T(8,128)(2,1)S(1)}, bf16[128,512]{1,0:T(8,128)(2,1)S(1)}, u32[]{:S(2)}, u32[]{:S(2)}) collective-permute-start(bf16[128,512]{1,0:T(8,128)(2,1)S(1)} %get-tuple-element.39), channel_id=1, source_target_pairs={{0,16},{16,32},{32,48},{48,64},{64,80},{80,96},{96,112},{112,0},{1... | collective-permute-start | bytes 393224 | tf_op jit(solution)/shard_map/ppermute | solution.py:28
  73.4 5.3 %collective-permute-start.5 = (bf16[128,512]{1,0:T(8,128)(2,1)S(1)}, bf16[128,512]{1,0:T(8,128)(2,1)S(1)}, u32[]{:S(2)}, u32[]{:S(2)}) collective-permute-start(bf16[128,512]{1,0:T(8,128)(2,1)S(1)} %get-tuple-element.39), channel_id=1, source_target_pairs={{0,112},{16,0},{32,16},{48,32},{64,48},{80,64},{96,80},{112,96},{1... | collective-permute-start | bytes 393224 | tf_op jit(solution)/shard_map/ppermute | solution.py:28
  76.4 6.8 %collective-permute-start.6 = (bf16[128,512]{1,0:T(8,128)(2,1)S(1)}, bf16[128,512]{1,0:T(8,128)(2,1)S(1)}, u32[]{:S(2)}, u32[]{:S(2)}) collective-permute-start(bf16[128,512]{1,0:T(8,128)(2,1)S(1)} %get-tuple-element.39), channel_id=1, source_target_pairs={{0,32},{16,48},{32,64},{48,80},{64,96},{80,112},{96,0},{112,16},{1... | collective-permute-start | bytes 393224 | tf_op jit(solution)/shard_map/ppermute | solution.py:28
  83.2 6.5 %collective-permute-start.7 = (bf16[512,512]{1,0:T(8,128)(2,1)S(1)}, bf16[512,512]{1,0:T(8,128)(2,1)S(1)}, u32[]{:S(2)}, u32[]{:S(2)}) collective-permute-start(bf16[512,512]{1,0:T(8,128)(2,1)S(1)} %constant_dynamic-update-slice_fusion.2.rest_0_), channel_id=1, source_target_pairs={{0,8},{8,0},{1,9},{9,1},{2,10},{10,2},{3,11},{11,3},{4,12},{12,4},... | collective-permute-start | bytes 1572872 | tf_op jit(solution)/shard_map/ppermute | solution.py:24
  87.3 19.9 %collective-permute-start.8 = (bf16[512,512]{1,0:T(8,128)(2,1)S(1)}, bf16[512,512]{1,0:T(8,128)(2,1)S(1)}, u32[]{:S(2)}, u32[]{:S(2)}) collective-permute-start(bf16[512,512]{1,0:T(8,128)(2,1)S(1)} %constant_dynamic-update-slice_fusion.2.rest_0_), channel_id=1, source_target_pairs={{0,128},{128,0},{1,129},{129,1},{2,130},{130,2},{3,131},{131,3},{4... | collective-permute-start | bytes 1572872 | tf_op jit(solution)/shard_map/ppermute | solution.py:24
  89.7 1.9 %copy-start.4 = (f32[1536,512]{1,0:T(8,128)S(1)}, f32[1536,512]{1,0:T(8,128)}, u32[]{:S(2)}) copy-start(f32[1536,512]{1,0:T(8,128)} %copy-done.3) | copy-start | bytes 9437188
  107.3 9.8 %collective-permute-start.9 = (bf16[512,512]{1,0:T(8,128)(2,1)S(1)}, bf16[512,512]{1,0:T(8,128)(2,1)S(1)}, u32[]{:S(2)}, u32[]{:S(2)}) collective-permute-start(bf16[512,512]{1,0:T(8,128)(2,1)S(1)} %collective-permute-done.8.rest_0_), channel_id=1, source_target_pairs={{0,8},{8,0},{1,9},{9,1},{2,10},{10,2},{3,11},{11,3},{4,12},{12,4},... | collective-permute-start | bytes 1572872 | tf_op jit(solution)/shard_map/ppermute | solution.py:24

commit v3 on v2

v3 whole, which is shorter than its diff:
```python
import functools

import jax
import jax.numpy as jnp
from jax import lax
from jax.experimental import pallas as pl
from jax.experimental.pallas import tpu as pltpu
from jax.sharding import Mesh, PartitionSpec as P

HD = 128
WINDOW = 1024
QSCALAR = 168
YH, NZ, NC, NH = 2, 8, 2, 8
SEQ = ("yh", "z", "core")
BAND_TILE = 256
TILE = 512
CHUNK = 256
NEG = -1e30
BIG = 1e30
VMEM_LIMIT = 24 * 1024 * 1024


def swapped(array, axis):
    return lax.ppermute(array, axis, [(0, 1), (1, 0)])


def round_z(array, r):
    return lax.ppermute(array, "z", [(i, (i + r) % NZ) for i in range(NZ)])


def pick(array, at):
    return lax.dynamic_index_in_dim(array, at, 0, keepdims=False)


def halved(part, axis, root_at):
    at = lax.axis_index(axis)
    part = part.reshape(2, part.shape[0] // 2, part.shape[1])
    came = swapped(pick(part, 1 - at), axis)
    return jnp.where(root_at == at, pick(part, at), came)


def normed(rows, gain, cosine, sine):
    mean_sq = jnp.mean(rows * rows, axis=-1, keepdims=True)
    rows = rows * lax.rsqrt(mean_sq + 1e-06) * gain
    return rows * cosine + pltpu.roll(rows, HD // 2, 1) * sine


def tables(cos_ref, sin_ref, at):
    cosine, sine = cos_ref[at, :], sin_ref[at, :]
    return jnp.concatenate([cosine, cosine], axis=1), jnp.concatenate([-sine, sine], axis=1)


def dot_t(a, b):
    return lax.dot_general(a, b, (((1,), (1,)), ((), ())), preferred_element_type=jnp.float32)


def rows_at(t, tile):
    return pl.ds(pl.multiple_of(t * tile, tile), tile)


def columns_of(h):
    return slice(h * HD, (h + 1) * HD)


def stacked(ref, at, heads):
    return jnp.concatenate([ref[at, columns_of(h)] for h in heads], axis=0)


def prep_kernel(q_ref, k_ref, qg_ref, kg_ref, cos_ref, sin_ref, qn_ref, kn_ref):
    local = q_ref.shape[0]

    def own(t, _):
        at = rows_at(t, BAND_TILE)
        cosine, sine = tables(cos_ref, sin_ref, rows_at(t + WINDOW // BAND_TILE, BAND_TILE))
        for c in range(k_ref.shape[1] // HD):
            rows = k_ref[at, columns_of(c)].astype(jnp.float32)
            kn_ref[at, columns_of(c)] = normed(rows, kg_ref[...], cosine, sine).astype(jnp.bfloat16)
        for h in range(q_ref.shape[1] // HD):
            rows = q_ref[at, columns_of(h)].astype(jnp.float32)
            rows = normed(rows, qg_ref[...], cosine, sine) * QSCALAR ** (-0.5)
            qn_ref[at, columns_of(h)] = rows.astype(jnp.bfloat16)
        return 0

    lax.fori_loop(0, local // BAND_TILE, own, 0)


def halo_kernel(k_ref, kg_ref, cos_ref, sin_ref, kn_ref):
    def one(t, _):
        at = rows_at(t, BAND_TILE)
        cosine, sine = tables(cos_ref, sin_ref, at)
        for c in range(kn_ref.shape[1] // HD):
            rows = k_ref[at, columns_of(c)].astype(jnp.float32)
            kn_ref[at, columns_of(c)] = normed(rows, kg_ref[...], cosine, sine).astype(jnp.bfloat16)
        return 0

    lax.fori_loop(0, WINDOW // BAND_TILE, one, 0)


def attend(state, query, key, value, keep_score=None, dead=None):
    score = dot_t(query, key)
    if keep_score is not None:
        score = jnp.where(keep_score, score, NEG)
    top = jnp.max(score, axis=1, keepdims=True)
    if dead is not None:
        top = jnp.where(dead, NEG, top)
    top = jnp.broadcast_to(top, query.shape)
    if state is not None:
        top = jnp.maximum(state[0], top)
    minus = top if dead is None else jnp.where(dead, BIG, top)
    weight = jnp.concatenate(
        [jnp.exp(score[:, i : i + HD] - minus).astype(jnp.bfloat16) for i in range(0, score.shape[1], HD)],
        axis=1,
    )
    value = jnp.concatenate([value, jnp.ones_like(value)], axis=1)
    out = jnp.dot(weight, value, preferred_element_type=jnp.float32)
    summed, total = out[:, :HD], out[:, HD:]
    if state is not None:
        keep = jnp.exp(state[0] - top)
        summed, total = state[1] * keep + summed, state[2] * keep + total
    return top, summed, total


def band_kernel(from_tile, first_ref, q_ref, kb_ref, vb_ref, k_ref, v_ref, top_ref, acc_ref, sum_ref):
    kv = k_ref.shape[1] // HD
    group = q_ref.shape[1] // HD // kv
    rows_in = lax.broadcasted_iota(jnp.int32, (group * BAND_TILE, CHUNK), 0) % BAND_TILE
    columns_in = lax.broadcasted_iota(jnp.int32, (group * BAND_TILE, CHUNK), 1)
    early = columns_in > rows_in
    late = columns_in <= rows_in
    reach = WINDOW // CHUNK
    is_first = first_ref[0] == 1
    for t in range(top_ref.shape[0] // BAND_TILE):
        block = from_tile + t
        at = slice(block * BAND_TILE, (block + 1) * BAND_TILE)
        to = slice(t * BAND_TILE, (t + 1) * BAND_TILE)
        queries = [stacked(q_ref, at, range(c * group, (c + 1) * group)) for c in range(kv)]
        state = [None] * kv
        for j in range(reach, -1, -1):
            e = block + j - reach
            mine = e >= 0
            keys_at = slice(e * CHUNK, (e + 1) * CHUNK) if mine else slice((e + reach) * CHUNK, (e + reach + 1) * CHUNK)
            for c in range(kv):
                state[c] = attend(
                    state[c],
                    queries[c],
                    (k_ref if mine else kb_ref)[keys_at, columns_of(c)],
                    v_ref[keys_at, columns_of(c)] if mine else vb_ref[keys_at, columns_of(kv + c)],
                    keep_score=late if j == reach else early if j == 0 else None,
                    dead=None if mine else is_first,
                )
        for c in range(kv):
            for g in range(group):
                rows = slice(g * BAND_TILE, (g + 1) * BAND_TILE)
                for ref, part in zip((top_ref, acc_ref, sum_ref), state[c]):
                    ref[to, columns_of(c * group + g)] = part[rows]


def prefix_kernel(last, bands, pieces, q_ref, *rest):
    states, rest = [rest[3 * i : 3 * i + 3] for i in range(bands)], rest[3 * bands :]
    p_refs, outs = rest[:pieces], rest[pieces:]
    tokens = p_refs[0].shape[0]
    kv = p_refs[0].shape[1] // (2 * HD)
    group = q_ref.shape[1] // HD // kv
    each = states[0][0].shape[0]

    def step(t, state_refs, at_in):
        at = rows_at(t, TILE)
        heads = [range(c * group, (c + 1) * group) for c in range(kv)]
        queries = [stacked(q_ref, at, heads[c]) for c in range(kv)]
        state = [tuple(stacked(ref, at_in, heads[c]) for ref in state_refs) for c in range(kv)]
        for p_ref in p_refs:
            for j in range(tokens // CHUNK):
                at_keys = slice(j * CHUNK, (j + 1) * CHUNK)
                for c in range(kv):
                    state[c] = attend(
                        state[c],
                        queries[c],
                        p_ref[at_keys, columns_of(2 * c)],
                        p_ref[at_keys, columns_of(2 * c + 1)],
                    )
        for c in range(kv):
            result = [(state[c][1] / state[c][2]).astype(jnp.bfloat16)] if last else state[c]
            for g in range(group):
                rows = slice(g * TILE, (g + 1) * TILE)
                for ref, part in zip(outs, result):
                    ref[at, columns_of(c * group + g)] = part[rows]

    if bands > 1:
        for i in range(q_ref.shape[0] // TILE):
            step(i, states[i * TILE // each], slice(i * TILE % each, i * TILE % each + TILE))
    else:

        def one(t, _):
            step(t, states[0], rows_at(t, TILE))
            return 0

        lax.fori_loop(0, q_ref.shape[0] // TILE, one, 0)


WHOLE = pl.BlockSpec(memory_space=pltpu.VMEM)
PARAMS = pltpu.CompilerParams(vmem_limit_bytes=VMEM_LIMIT)


def cost(pairs, in_out):
    return pl.CostEstimate(flops=8 * pairs * HD, transcendentals=pairs, bytes_accessed=in_out)


def normed_part(kernel, outs, *args):
    size = sum(o.size for o in outs)
    return pl.pallas_call(
        kernel,
        out_shape=outs,
        in_specs=[WHOLE] * len(args),
        out_specs=(WHOLE,) * len(outs),
        compiler_params=PARAMS,
        cost_estimate=pl.CostEstimate(flops=60 * size, transcendentals=size // HD, bytes_accessed=6 * size),
        name="norm_rope",
    )(*args)


def band_part(from_tile, tiles, first, q, key_before, before, k, v):
    width = q.shape[1]
    rows = tiles * BAND_TILE
    return pl.pallas_call(
        functools.partial(band_kernel, from_tile),
        out_shape=(jax.ShapeDtypeStruct((rows, width), jnp.float32),) * 3,
        in_specs=[pl.BlockSpec(memory_space=pltpu.SMEM)] + [WHOLE] * 5,
        out_specs=(WHOLE,) * 3,
        compiler_params=PARAMS,
        cost_estimate=cost(rows * (width // HD) * (WINDOW + BAND_TILE), 6 << 20),
        name="band",
    )(first, q, key_before, before, k, v)


def prefix_part(last, q, states, *pieces):
    local, width = q.shape
    flat = [part for state in states for part in state]
    if last:
        out_shape = jax.ShapeDtypeStruct((local, width), jnp.bfloat16)
        out_specs = WHOLE
    else:
        out_shape = (jax.ShapeDtypeStruct((local, width), jnp.float32),) * 3
        out_specs = (WHOLE,) * 3
    return pl.pallas_call(
        functools.partial(prefix_kernel, last, len(states), len(pieces)),
        out_shape=out_shape,
        in_specs=[WHOLE] * (1 + len(flat) + len(pieces)),
        out_specs=out_specs,
        compiler_params=PARAMS,
        cost_estimate=cost(local * (width // HD) * len(pieces) * pieces[0].shape[0], 10 << 20),
        name="prefix_last" if last else "prefix",
    )(q, *flat, *pieces)


def on_device(queries, keys, values, q_gain, k_gain, positions, prefix_cache, owner):
    local = queries.shape[0]
    root = owner[0]
    root_y, root_z, root_c = root // (NZ * NC), (root // NC) % NZ, root % NC
    q_gain, k_gain = (1.0 + q_gain)[None], (1.0 + k_gain)[None]
    first = (lax.axis_index(SEQ) == 0).astype(jnp.int32).reshape(1)

    slab = halved(prefix_cache[0], "core", root_c)
    onward = [(i, i + 1) for i in range(YH * NZ * NC - 1)]
    tail = jnp.concatenate([keys[local - WINDOW :], values[local - WINDOW :]], axis=1)
    slab, tail = lax.optimization_barrier((slab, tail))
    before = lax.ppermute(tail, SEQ, onward)
    slab = halved(slab, "yh", root_y)

    half = HD // 2
    freq = 10000.0 ** (-(jnp.arange(half).astype(jnp.float32) * 2.0) / HD)
    extended = positions[0] + jnp.arange(-WINDOW, local, dtype=jnp.int32)
    angle = extended.astype(jnp.float32)[:, None] * freq[None, :]
    cosine, sine = jnp.cos(angle), jnp.sin(angle)
    query, key = normed_part(
        prep_kernel,
        (
            jax.ShapeDtypeStruct(queries.shape, jnp.bfloat16),
            jax.ShapeDtypeStruct(keys.shape, jnp.bfloat16),
        ),
        queries, keys, q_gain, k_gain, cosine, sine,
    )
    slab, query = lax.optimization_barrier((slab, query))

    rows, wide = slab.shape
    parts = slab.reshape(NZ, rows // NZ, NH, wide // NH).transpose(0, 2, 1, 3)
    parts = parts.reshape(NZ * NH, rows // NZ, wide // NH)
    parts = lax.all_to_all(parts, ("z", "head"), split_axis=0, concat_axis=0, tiled=True)
    (key_before,) = normed_part(
        halo_kernel,
        (jax.ShapeDtypeStruct((WINDOW, keys.shape[1]), jnp.bfloat16),),
        before, k_gain, cosine, sine,
    )

    def band(at, first):
        return band_part(2 * at, 2, first, query, key_before, before, key, values)

    states = [band(0, first)]
    parts, top = lax.optimization_barrier((parts, states[0][0]))
    states[0] = (top, *states[0][1:])
    mine = pick(parts.reshape(NZ, NH, rows // NZ, wide // NH), root_z)
    mine = mine.reshape(NH * rows // NZ, wide // NH)
    mine, first = lax.optimization_barrier((mine, first))

    across = round_z(mine, NZ // 2)
    states.append(band(1, first))
    across, top = lax.optimization_barrier((across, states[1][0]))
    states[1] = (top, *states[1][1:])
    mine = jnp.concatenate([mine, across], axis=0)
    mine, first = lax.optimization_barrier((mine, first))

    around = [round_z(mine, 1), round_z(mine, -1), round_z(mine, 2)]
    states.append(band(2, first))
    around, top = lax.optimization_barrier((around, states[2][0]))
    states[2] = (top, *states[2][1:])
    mine = jnp.concatenate([mine, *around], axis=0)

    far = swapped(mine, "yh")
    state = prefix_part(False, query, states, mine, swapped(mine, "core"))
    far, top = lax.optimization_barrier((far, state[0]))
    last = swapped(far, "core")
    state = prefix_part(False, query, [(top, *state[1:])], far)
    return prefix_part(True, query, [state], last)


def solution(mesh):
    fine = Mesh(mesh.devices.reshape(YH, NZ, NC, NH), SEQ + ("head",))
    return jax.shard_map(
        on_device,
        mesh=fine,
        in_specs=(
            P(SEQ, "head"),
            P(SEQ, "head"),
            P(SEQ, "head"),
            P(),
            P(),
            P(SEQ),
            P(SEQ, "head", None),
            P(),
        ),
        out_specs=P(SEQ, "head"),
        check_vma=False,
    )
```

time: 127 us -> 109 us (0.86)
  Pallas kernels: 54.3 us -> 42 us
  starting transfers between devices: 37.4 us -> 31 us
  waiting for transfers between devices: 8.6 us -> 14.4 us
  other arithmetic: 12.6 us -> 8.7 us
  local copies, waits for them, and re-layouts: 13 us -> 10.8 us
    pallas_call x5 -> x8, Pallas kernels: 54.3 us -> 42 us  [the longest x3 18.5 us: prefix_part(): pl.pallas_call(functools.partial(prefix_kernel, last, len(states), len(pi...]
    all_to_all x1, waiting for transfers between devices: 0.01 us -> 6.52 us  [on_device(): lax.all_to_all(parts, ('z', 'head'), split_axis=0, concat_axis=0, tiled=T...]
    ppermute x4, waiting for transfers between devices: 8.58 us -> 2.39 us  [round_z(): return lax.ppermute(array, 'z', [(i, (i + r) % NZ) for i in range(NZ)])]
    neg x1 -> x0, other arithmetic: 5.99 us -> none  [on_device(): sine = jnp.concatenate([-sine, sine], axis=1)]
    ppermute x5, waiting for transfers between devices: 0.01 us -> 5.53 us  [swapped(): return lax.ppermute(array, axis, [(0, 1), (1, 0)])]
    sin x0 -> x1, other arithmetic: none -> 4.58 us  [on_device(): cosine, sine = (jnp.cos(angle), jnp.sin(angle))]
    concatenate x1, other arithmetic: 4.04 us -> 0.01 us  [on_device(): mine = jnp.concatenate([mine, across], axis=0)]
    ppermute x1, starting transfers between devices: 5.14 us -> 2.49 us  [on_device(): before = lax.ppermute(tail, SEQ, onward)]
  transfers between devices with their start and end apart: 11 -> 11, of which waited for: 3 -> 4; matrix products, arithmetic and copies ran while one was open for 13% -> 8% of each run, Pallas kernels for 35% -> 33%
where the time goes in v3:
time: 109 us; the launch traced here: 108 us
  Pallas kernels  42 us (39%)
  starting transfers between devices  31 us (28%)
  waiting for transfers between devices  14.4 us (13%)
  local copies, waits for them, and re-layouts  10.8 us (10%)
  other arithmetic  8.7 us (8%)
  between operations  1.1 us (1%)
    pallas_call x3, Pallas kernels, prefix_part(): pl.pallas_call(functools.partial(prefix_kernel, last, len(states), len(pi...  18.5 us
    pallas_call x3, Pallas kernels, band_part(): pl.pallas_call(functools.partial(band_kernel, from_tile), out_shape=(jax....  14.9 us
    all_to_all x1, starting transfers between devices, on_device(): lax.all_to_all(parts, ('z', 'head'), split_axis=0, concat_axis=0, tiled=T...  11.6 us
    ppermute x5, starting transfers between devices, swapped(): return lax.ppermute(array, axis, [(0, 1), (1, 0)])  9.47 us
    pallas_call x2, Pallas kernels, normed_part(): pl.pallas_call(kernel, out_shape=outs, in_specs=[WHOLE] * len(args), out_...  8.61 us
    ppermute x4, starting transfers between devices, round_z(): return lax.ppermute(array, 'z', [(i, (i + r) % NZ) for i in range(NZ)])  7.41 us
    all_to_all x1, waiting for transfers between devices, on_device(): lax.all_to_all(parts, ('z', 'head'), split_axis=0, concat_axis=0, tiled=T...  6.52 us
    unnamed x41, local copies, waits for them, and re-layouts  6.24 us
  transfers between devices with their start and end apart: 11, of which 4 were waited for; matrix products, arithmetic and copies ran while one was open for 8% of the time, Pallas kernels for 33%

profile of v3, /device:TPU:1, one launch (start us, length us, event | category | flops | bytes accessed | tf_op | source)
XLA Modules:
  0.0 108.1 jit_solution(6772617019674502369)
XLA Ops:
  0.0 2.4 %dynamic-slice_bitcast_fusion = bf16[128,4096]{1,0:T(8,128)(2,1)} fusion(bf16[2,128,4096]{2,1,0:T(8,128)(2,1)} %bitcast.31, s32[]{:T(128)S(6)} %select_n.57), kind=kLoop, calls=%fused_computation.4 | loop fusion | bytes 2097156 | tf_op jit(solution)/shard_map/jit(dynamic_index_in_dim)/squeeze | solution.py:32
  2.4 3.2 %collective-permute-start = (bf16[128,4096]{1,0:T(8,128)(2,1)}, bf16[128,4096]{1,0:T(8,128)(2,1)}, u32[]{:S(2)}, u32[]{:S(2)}) collective-permute-start(bf16[128,4096]{1,0:T(8,128)(2,1)} %dynamic-slice_bitcast_fusion), channel_id=1, source_target_pairs={{0,8},{8,0},{1,9},{9,1},{2,10},{10,2},{3,11},{11,3},{4,12},{12,4},... | collective-permute-start | bytes 3145736 | tf_op jit(solution)/shard_map/ppermute | solution.py:24
  6.3 1.3 %slice.11 = s32[1]{0:T(128)} slice(s32[1536]{0:T(1024)} %param.13), slice={[0:1]} | slice | bytes 8 | tf_op jit(solution)/shard_map/slice | solution.py:271
  9.5 1.3 %bitcast_select_fusion = bf16[128,4096]{1,0:T(8,128)(2,1)S(1)} fusion(bf16[128,4096]{1,0:T(8,128)(2,1)} %collective-permute-done, bf16[2,128,4096]{2,1,0:T(8,128)(2,1)S(1)} %bitcast.32, s32[]{:T(128)S(6)} %select_n.56, pred[]{:T(512)S(6)} %eq.13), kind=kLoop, calls=%fused_computation.3 | loop fusion | flops 524288 | bytes 3145733 | tf_op jit(solution)/shard_map/jit(_where)/select_n | solution.py:39
  11.0 1.3 %collective-permute-start.1 = (bf16[64,4096]{1,0:T(8,128)(2,1)S(1)}, bf16[64,4096]{1,0:T(8,128)(2,1)S(1)}, u32[]{:S(2)}, u32[]{:S(2)}) collective-permute-start(bf16[64,4096]{1,0:T(8,128)(2,1)S(1)} %dynamic-slice_bitcast_fusion.1), channel_id=1, source_target_pairs={{0,128},{128,0},{1,129},{129,1},{2,130},{130,2},{3,131},{131,3},{4... | collective-permute-start | bytes 1572872 | tf_op jit(solution)/shard_map/ppermute | solution.py:24
  12.2 4.6 %multiply_sine_fusion = (f32[2560,64]{1,0:T(8,128)S(1)}, f32[2560,64]{1,0:T(8,128)S(1)}) fusion(f32[64]{0:T(128)S(1)} %multiply_power_fusion, f32[2560]{0:T(1024)S(1)} %add_convert_fusion), kind=kLoop, calls=%fused_computation | loop fusion | flops 163840 | bytes 1321216 | tf_op jit(solution)/shard_map/sin | solution.py:273
  16.8 5.6 %norm_rope.2 = (bf16[1536,512]{1,0:T(8,128)(2,1)S(1)}, bf16[1536,256]{1,0:T(8,128)(2,1)S(1)}) custom-call(bf16[1536,512]{1,0:T(8,128)(2,1)S(1)} %copy-done.4, bf16[1536,256]{1,0:T(8,128)(2,1)S(1)} %copy-done, f32[1,128]{1,0:T(1,128)S(1)} %add_bitcast_fusion.1.qg_ref, f32[1,128]{1,0:T(1,128)S(1)} %add_bitcast_fusion.kg_ref, ...), custom_call_target="tpu_custom_call" | custom-call | flops 70778880 | bytes 7077888 | tf_op jit(solution)/shard_map/norm_rope/pallas_call | solution.py:210
  24.5 2.5 %collective-permute-start.2 = (bf16[1024,512]{1,0:T(8,128)(2,1)}, bf16[1024,512]{1,0:T(8,128)(2,1)}, u32[]{:S(2)}, u32[]{:S(2)}) collective-permute-start(bf16[1024,512]{1,0:T(8,128)(2,1)} %pad_maximum_fusion), channel_id=1, source_target_pairs={{0,8},{8,16},{16,24},{24,32},{32,40},{40,48},{48,56},{56,64},{64,7... | collective-permute-start | bytes 3145736 | tf_op jit(solution)/shard_map/ppermute | solution.py:266
  27.9 11.6 %all-to-all-start = ((bf16[64,8,512]{2,1,0:T(8,128)(2,1)}), bf16[64,8,512]{2,1,0:T(8,128)(2,1)}, u32[]{:S(2)}, u32[]{:S(2)}) async-start(bf16[64,8,512]{2,1,0:T(8,128)(2,1)} %bitcast.12), calls=%async_computation | async-start | bytes 1048576 | tf_op jit(solution)/shard_map/all_to_all | solution.py:287
  39.7 3.0 %norm_rope.3.kb_ref = bf16[1024,256]{1,0:T(8,128)(2,1)S(1)} custom-call(bf16[1024,512]{1,0:T(8,128)(2,1)} %collective-permute-done.2.k_ref.vb_ref, f32[1,128]{1,0:T(1,128)S(1)} %add_bitcast_fusion.kg_ref, f32[2560,64]{1,0:T(8,128)S(1)} %get-tuple-element.76.cos_ref, f32[2560,64]{1,0:T(8,128)S(1)} %get-tuple-element.75.sin_ref), custom_call_target="tpu_custom_call" | custom-call | flops 15728640 | bytes 1572864 | tf_op jit(solution)/shard_map/norm_rope/pallas_call | solution.py:210
  42.7 5.3 %band.3 = (f32[512,512]{1,0:T(8,128)S(1)}, f32[512,512]{1,0:T(8,128)S(1)}, f32[512,512]{1,0:T(8,128)S(1)}) custom-call(s32[1]{0:T(128)} %bitcast.13.first_ref, bf16[1536,512]{1,0:T(8,128)(2,1)S(1)} %copy-done.2, bf16[1024,256]{1,0:T(8,128)(2,1)S(1)} %norm_rope.3.kb_ref, bf16[1024,512]{1,0:T(8,128)(2,1)} %collective-permute-done.2.k_ref.vb_ref, ...), custom_call_target="tpu_custom_call" | custom-call | flops 2684354560 | bytes 6291456 | tf_op jit(solution)/shard_map/band/pallas_call | solution.py:224
  51.0 6.5 %all-to-all-done = bf16[64,8,512]{2,1,0:T(8,128)(2,1)} async-done(((bf16[64,8,512]{2,1,0:T(8,128)(2,1)}), bf16[64,8,512]{2,1,0:T(8,128)(2,1)}, u32[]{:S(2)}, u32[]{:S(2)}) %all-to-all-start) | async-done | bytes 524320 | tf_op jit(solution)/shard_map/all_to_all | solution.py:287
  58.3 3.2 %collective-permute-start.3 = (bf16[64,512]{1,0:T(8,128)(2,1)S(1)}, bf16[64,512]{1,0:T(8,128)(2,1)S(1)}, u32[]{:S(2)}, u32[]{:S(2)}) collective-permute-start(bf16[64,512]{1,0:T(8,128)(2,1)S(1)} %dynamic-slice_bitcast_fusion.2), channel_id=1, source_target_pairs={{0,64},{16,80},{32,96},{48,112},{64,0},{80,16},{96,32},{112,48},{1... | collective-permute-start | bytes 196616 | tf_op jit(solution)/shard_map/ppermute | solution.py:28
  62.7 4.9 %band.4 = (f32[512,512]{1,0:T(8,128)S(1)}, f32[512,512]{1,0:T(8,128)S(1)}, f32[512,512]{1,0:T(8,128)S(1)}) custom-call(s32[1]{0:T(128)} %bitcast.13.first_ref, bf16[1536,512]{1,0:T(8,128)(2,1)S(1)} %copy-done.3, bf16[1024,256]{1,0:T(8,128)(2,1)S(1)} %norm_rope.3.kb_ref, bf16[1024,512]{1,0:T(8,128)(2,1)} %collective-permute-done.2.k_ref.vb_ref, ...), custom_call_target="tpu_custom_call" | custom-call | flops 2684354560 | bytes 6291456 | tf_op jit(solution)/shard_map/band/pallas_call | solution.py:224
  67.7 2.7 %collective-permute-start.6 = (bf16[128,512]{1,0:T(8,128)(2,1)S(1)}, bf16[128,512]{1,0:T(8,128)(2,1)S(1)}, u32[]{:S(2)}, u32[]{:S(2)}) collective-permute-start(bf16[128,512]{1,0:T(8,128)(2,1)S(1)} %pad_maximum_fusion.1), channel_id=1, source_target_pairs={{0,32},{16,48},{32,64},{48,80},{64,96},{80,112},{96,0},{112,16},{1... | collective-permute-start | bytes 393224 | tf_op jit(solution)/shard_map/ppermute | solution.py:28
  70.6 1.2 %collective-permute-start.4 = (bf16[128,512]{1,0:T(8,128)(2,1)S(1)}, bf16[128,512]{1,0:T(8,128)(2,1)S(1)}, u32[]{:S(2)}, u32[]{:S(2)}) collective-permute-start(bf16[128,512]{1,0:T(8,128)(2,1)S(1)} %pad_maximum_fusion.1), channel_id=1, source_target_pairs={{0,16},{16,32},{32,48},{48,64},{64,80},{80,96},{96,112},{112,0},{1... | collective-permute-start | bytes 393224 | tf_op jit(solution)/shard_map/ppermute | solution.py:28
  71.9 4.7 %band.5 = (f32[512,512]{1,0:T(8,128)S(1)}, f32[512,512]{1,0:T(8,128)S(1)}, f32[512,512]{1,0:T(8,128)S(1)}) custom-call(s32[1]{0:T(128)} %bitcast.13.first_ref, bf16[1536,512]{1,0:T(8,128)(2,1)S(1)} %copy-done.3, bf16[1024,256]{1,0:T(8,128)(2,1)S(1)} %norm_rope.3.kb_ref, bf16[1024,512]{1,0:T(8,128)(2,1)} %collective-permute-done.2.k_ref.vb_ref, ...), custom_call_target="tpu_custom_call" | custom-call | flops 2684354560 | bytes 6291456 | tf_op jit(solution)/shard_map/band/pallas_call | solution.py:224
  76.6 2.4 %collective-permute-done.4 = bf16[128,512]{1,0:T(8,128)(2,1)S(1)} collective-permute-done((bf16[128,512]{1,0:T(8,128)(2,1)S(1)}, bf16[128,512]{1,0:T(8,128)(2,1)S(1)}, u32[]{:S(2)}, u32[]{:S(2)}) %collective-permute-start.4) | collective-permute-done | bytes 131104 | tf_op jit(solution)/shard_map/ppermute | solution.py:28
  79.0 2.5 %collective-permute-start.8 = (bf16[512,512]{1,0:T(8,128)(2,1)S(1)}, bf16[512,512]{1,0:T(8,128)(2,1)S(1)}, u32[]{:S(2)}, u32[]{:S(2)}) collective-permute-start(bf16[512,512]{1,0:T(8,128)(2,1)S(1)} %constant_dynamic-update-slice_fusion.rest_9_), channel_id=1, source_target_pairs={{0,8},{8,0},{1,9},{9,1},{2,10},{10,2},{3,11},{11,3},{4,12},{12,4},... | collective-permute-start | bytes 1572872 | tf_op jit(solution)/shard_map/ppermute | solution.py:24
  81.5 1.4 %collective-permute-start.7 = (bf16[512,512]{1,0:T(8,128)(2,1)S(1)}, bf16[512,512]{1,0:T(8,128)(2,1)S(1)}, u32[]{:S(2)}, u32[]{:S(2)}) collective-permute-start(bf16[512,512]{1,0:T(8,128)(2,1)S(1)} %constant_dynamic-update-slice_fusion.rest_9_), channel_id=1, source_target_pairs={{0,128},{128,0},{1,129},{129,1},{2,130},{130,2},{3,131},{131,3},{4... | collective-permute-start | bytes 1572872 | tf_op jit(solution)/shard_map/ppermute | solution.py:24
  83.0 7.8 %prefix.2 = (f32[1536,512]{1,0:T(8,128)S(1)}, f32[1536,512]{1,0:T(8,128)S(1)}, f32[1536,512]{1,0:T(8,128)S(1)}) custom-call(bf16[1536,512]{1,0:T(8,128)(2,1)S(1)} %copy-done.3, f32[512,512]{1,0:T(8,128)S(1)} %copy-done.11, f32[512,512]{1,0:T(8,128)S(1)} %copy-done.13, f32[512,512]{1,0:T(8,128)S(1)} %copy-done.15, f32[512,512]{1,0:T(8,128)S(1)} %get-tuple-element.61.rest_3_, ...), custom_call_target="tpu_custom_call" | custom-call | flops 6442450944 | bytes 10485760 | tf_op jit(solution)/shard_map/prefix/pallas_call | solution.py:244
  90.8 5.3 %collective-permute-done.7.rest_3_ = bf16[512,512]{1,0:T(8,128)(2,1)S(1)} collective-permute-done((bf16[512,512]{1,0:T(8,128)(2,1)S(1)}, bf16[512,512]{1,0:T(8,128)(2,1)S(1)}, u32[]{:S(2)}, u32[]{:S(2)}) %collective-permute-start.7) | collective-permute-done | bytes 524320 | tf_op jit(solution)/shard_map/ppermute | solution.py:24
  97.3 4.7 %prefix.3 = (f32[1536,512]{1,0:T(8,128)S(1)}, f32[1536,512]{1,0:T(8,128)S(1)}, f32[1536,512]{1,0:T(8,128)S(1)}) custom-call(bf16[1536,512]{1,0:T(8,128)(2,1)S(1)} %copy-done.3, f32[1536,512]{1,0:T(8,128)S(1)} %get-tuple-element.68.rest_0_, f32[1536,512]{1,0:T(8,128)S(1)} %get-tuple-element.69.rest_1_, f32[1536,512]{1,0:T(8,128)S(1)} %get-tuple-element.70.rest_2_, ...), custom_call_target="tpu_custom_call" | custom-call | flops 3221225472 | bytes 10485760 | tf_op jit(solution)/shard_map/prefix/pallas_call | solution.py:244
  102.1 6.0 %prefix_last.1 = bf16[1536,512]{1,0:T(8,128)(2,1)} custom-call(bf16[1536,512]{1,0:T(8,128)(2,1)S(1)} %copy-done.3, f32[1536,512]{1,0:T(8,128)S(1)} %get-tuple-element.72.rest_0_, f32[1536,512]{1,0:T(8,128)S(1)} %get-tuple-element.73.rest_1_, f32[1536,512]{1,0:T(8,128)S(1)} %get-tuple-element.74.rest_2_, bf16[512,512]{1,0:T(8,128)(2,1)S(1)} %collective-permute-done.9.rest_3_), custom_call_target="tpu_custom_call" | custom-call | flops 3221225472 | bytes 10485760 | tf_op jit(solution)/shard_map/prefix_last/pallas_call | solution.py:244
  (65 shorter events, 11.5 us)
Async XLA Ops:
  0.0 8.4 %slice-start = ((bf16[1536,256]{1,0:T(8,128)(2,1)}), bf16[1024,256]{1,0:T(8,128)(2,1)S(1)}, s32[]{:S(2)}) async-start(bf16[1536,256]{1,0:T(8,128)(2,1)} %k_ref.1), calls=%async_computation.1 | async-start | bytes 1048576 | tf_op jit(solution)/shard_map/slice | solution.py:264
  0.0 8.4 %slice-start.1 = ((bf16[1536,256]{1,0:T(8,128)(2,1)}), bf16[1024,256]{1,0:T(8,128)(2,1)S(1)}, s32[]{:S(2)}) async-start(bf16[1536,256]{1,0:T(8,128)(2,1)} %v_ref.5), calls=%async_computation.2 | async-start | bytes 1048576 | tf_op jit(solution)/shard_map/slice | solution.py:264
  2.4 7.1 %collective-permute-start = (bf16[128,4096]{1,0:T(8,128)(2,1)}, bf16[128,4096]{1,0:T(8,128)(2,1)}, u32[]{:S(2)}, u32[]{:S(2)}) collective-permute-start(bf16[128,4096]{1,0:T(8,128)(2,1)} %dynamic-slice_bitcast_fusion), channel_id=1, source_target_pairs={{0,8},{8,0},{1,9},{9,1},{2,10},{10,2},{3,11},{11,3},{4,12},{12,4},... | collective-permute-start | bytes 3145736 | tf_op jit(solution)/shard_map/ppermute | solution.py:24
  7.6 1.9 %copy-start.16 = (bf16[1,256,4096]{2,1,0:T(8,128)(2,1)S(1)}, bf16[1,256,4096]{2,1,0:T(8,128)(2,1)}, u32[]{:S(2)}) copy-start(bf16[1,256,4096]{2,1,0:T(8,128)(2,1)} %param.14) | copy-start | bytes 6291460
  10.9 5.9 %copy-start = (bf16[1536,256]{1,0:T(8,128)(2,1)S(1)}, bf16[1536,256]{1,0:T(8,128)(2,1)}, u32[]{:S(2)}) copy-start(bf16[1536,256]{1,0:T(8,128)(2,1)} %k_ref.1) | copy-start | bytes 2359300
  10.9 5.9 %copy-start.4 = (bf16[1536,512]{1,0:T(8,128)(2,1)S(1)}, bf16[1536,512]{1,0:T(8,128)(2,1)}, u32[]{:S(2)}) copy-start(bf16[1536,512]{1,0:T(8,128)(2,1)} %q_ref.1) | copy-start | bytes 4718596
  11.0 16.1 %collective-permute-start.1 = (bf16[64,4096]{1,0:T(8,128)(2,1)S(1)}, bf16[64,4096]{1,0:T(8,128)(2,1)S(1)}, u32[]{:S(2)}, u32[]{:S(2)}) collective-permute-start(bf16[64,4096]{1,0:T(8,128)(2,1)S(1)} %dynamic-slice_bitcast_fusion.1), channel_id=1, source_target_pairs={{0,128},{128,0},{1,129},{129,1},{2,130},{130,2},{3,131},{131,3},{4... | collective-permute-start | bytes 1572872 | tf_op jit(solution)/shard_map/ppermute | solution.py:24
  24.5 15.1 %collective-permute-start.2 = (bf16[1024,512]{1,0:T(8,128)(2,1)}, bf16[1024,512]{1,0:T(8,128)(2,1)}, u32[]{:S(2)}, u32[]{:S(2)}) collective-permute-start(bf16[1024,512]{1,0:T(8,128)(2,1)} %pad_maximum_fusion), channel_id=1, source_target_pairs={{0,8},{8,16},{16,24},{24,32},{32,40},{40,48},{48,56},{56,64},{64,7... | collective-permute-start | bytes 3145736 | tf_op jit(solution)/shard_map/ppermute | solution.py:266
  27.9 29.6 %all-to-all-start = ((bf16[64,8,512]{2,1,0:T(8,128)(2,1)}), bf16[64,8,512]{2,1,0:T(8,128)(2,1)}, u32[]{:S(2)}, u32[]{:S(2)}) async-start(bf16[64,8,512]{2,1,0:T(8,128)(2,1)} %bitcast.12), calls=%async_computation | async-start | bytes 1048576 | tf_op jit(solution)/shard_map/all_to_all | solution.py:287
  39.6 3.0 %copy-start.2 = (bf16[1536,512]{1,0:T(8,128)(2,1)S(1)}, bf16[1536,512]{1,0:T(8,128)(2,1)}, u32[]{:S(2)}) copy-start(bf16[1536,512]{1,0:T(8,128)(2,1)} %copy-done.1) | copy-start | bytes 4718596
  39.6 3.0 %copy-start.5 = (bf16[1536,256]{1,0:T(8,128)(2,1)S(1)}, bf16[1536,256]{1,0:T(8,128)(2,1)}, u32[]{:S(2)}) copy-start(bf16[1536,256]{1,0:T(8,128)(2,1)} %v_ref.5) | copy-start | bytes 2359300
  39.6 3.0 %copy-start.8 = (bf16[1536,256]{1,0:T(8,128)(2,1)S(1)}, bf16[1536,256]{1,0:T(8,128)(2,1)}, u32[]{:S(2)}) copy-start(bf16[1536,256]{1,0:T(8,128)(2,1)} %copy-done.7) | copy-start | bytes 2359300
  42.7 18.9 %copy-start.3 = (bf16[1536,512]{1,0:T(8,128)(2,1)S(1)}, bf16[1536,512]{1,0:T(8,128)(2,1)}, u32[]{:S(2)}) copy-start(bf16[1536,512]{1,0:T(8,128)(2,1)} %copy-done.1) | copy-start | bytes 4718596
  42.7 18.9 %copy-start.6 = (bf16[1536,256]{1,0:T(8,128)(2,1)S(1)}, bf16[1536,256]{1,0:T(8,128)(2,1)}, u32[]{:S(2)}) copy-start(bf16[1536,256]{1,0:T(8,128)(2,1)} %v_ref.5) | copy-start | bytes 2359300
  58.3 9.3 %collective-permute-start.3 = (bf16[64,512]{1,0:T(8,128)(2,1)S(1)}, bf16[64,512]{1,0:T(8,128)(2,1)S(1)}, u32[]{:S(2)}, u32[]{:S(2)}) collective-permute-start(bf16[64,512]{1,0:T(8,128)(2,1)S(1)} %dynamic-slice_bitcast_fusion.2), channel_id=1, source_target_pairs={{0,64},{16,80},{32,96},{48,112},{64,0},{80,16},{96,32},{112,48},{1... | collective-permute-start | bytes 196616 | tf_op jit(solution)/shard_map/ppermute | solution.py:28
  67.7 15.4 %copy-start.11 = (f32[512,512]{1,0:T(8,128)S(1)}, f32[512,512]{1,0:T(8,128)}, u32[]{:S(2)}) copy-start(f32[512,512]{1,0:T(8,128)} %copy-done.10) | copy-start | bytes 3145732
  67.7 15.4 %copy-start.13 = (f32[512,512]{1,0:T(8,128)S(1)}, f32[512,512]{1,0:T(8,128)}, u32[]{:S(2)}) copy-start(f32[512,512]{1,0:T(8,128)} %copy-done.12) | copy-start | bytes 3145732
  67.7 15.4 %copy-start.15 = (f32[512,512]{1,0:T(8,128)S(1)}, f32[512,512]{1,0:T(8,128)}, u32[]{:S(2)}) copy-start(f32[512,512]{1,0:T(8,128)} %copy-done.14) | copy-start | bytes 3145732
  67.7 8.9 %collective-permute-start.6 = (bf16[128,512]{1,0:T(8,128)(2,1)S(1)}, bf16[128,512]{1,0:T(8,128)(2,1)S(1)}, u32[]{:S(2)}, u32[]{:S(2)}) collective-permute-start(bf16[128,512]{1,0:T(8,128)(2,1)S(1)} %pad_maximum_fusion.1), channel_id=1, source_target_pairs={{0,32},{16,48},{32,64},{48,80},{64,96},{80,112},{96,0},{112,16},{1... | collective-permute-start | bytes 393224 | tf_op jit(solution)/shard_map/ppermute | solution.py:28
  70.4 6.2 %collective-permute-start.5 = (bf16[128,512]{1,0:T(8,128)(2,1)S(1)}, bf16[128,512]{1,0:T(8,128)(2,1)S(1)}, u32[]{:S(2)}, u32[]{:S(2)}) collective-permute-start(bf16[128,512]{1,0:T(8,128)(2,1)S(1)} %pad_maximum_fusion.1), channel_id=1, source_target_pairs={{0,112},{16,0},{32,16},{48,32},{64,48},{80,64},{96,80},{112,96},{1... | collective-permute-start | bytes 393224 | tf_op jit(solution)/shard_map/ppermute | solution.py:28
  70.6 8.3 %collective-permute-start.4 = (bf16[128,512]{1,0:T(8,128)(2,1)S(1)}, bf16[128,512]{1,0:T(8,128)(2,1)S(1)}, u32[]{:S(2)}, u32[]{:S(2)}) collective-permute-start(bf16[128,512]{1,0:T(8,128)(2,1)S(1)} %pad_maximum_fusion.1), channel_id=1, source_target_pairs={{0,16},{16,32},{32,48},{48,64},{64,80},{80,96},{96,112},{112,0},{1... | collective-permute-start | bytes 393224 | tf_op jit(solution)/shard_map/ppermute | solution.py:28
  79.0 4.0 %collective-permute-start.8 = (bf16[512,512]{1,0:T(8,128)(2,1)S(1)}, bf16[512,512]{1,0:T(8,128)(2,1)S(1)}, u32[]{:S(2)}, u32[]{:S(2)}) collective-permute-start(bf16[512,512]{1,0:T(8,128)(2,1)S(1)} %constant_dynamic-update-slice_fusion.rest_9_), channel_id=1, source_target_pairs={{0,8},{8,0},{1,9},{9,1},{2,10},{10,2},{3,11},{11,3},{4,12},{12,4},... | collective-permute-start | bytes 1572872 | tf_op jit(solution)/shard_map/ppermute | solution.py:24
  81.5 14.7 %collective-permute-start.7 = (bf16[512,512]{1,0:T(8,128)(2,1)S(1)}, bf16[512,512]{1,0:T(8,128)(2,1)S(1)}, u32[]{:S(2)}, u32[]{:S(2)}) collective-permute-start(bf16[512,512]{1,0:T(8,128)(2,1)S(1)} %constant_dynamic-update-slice_fusion.rest_9_), channel_id=1, source_target_pairs={{0,128},{128,0},{1,129},{129,1},{2,130},{130,2},{3,131},{131,3},{4... | collective-permute-start | bytes 1572872 | tf_op jit(solution)/shard_map/ppermute | solution.py:24
  96.2 5.9 %collective-permute-start.9 = (bf16[512,512]{1,0:T(8,128)(2,1)S(1)}, bf16[512,512]{1,0:T(8,128)(2,1)S(1)}, u32[]{:S(2)}, u32[]{:S(2)}) collective-permute-start(bf16[512,512]{1,0:T(8,128)(2,1)S(1)} %collective-permute-done.7.rest_3_), channel_id=1, source_target_pairs={{0,8},{8,0},{1,9},{9,1},{2,10},{10,2},{3,11},{11,3},{4,12},{12,4},... | collective-permute-start | bytes 1572872 | tf_op jit(solution)/shard_map/ppermute | solution.py:24
  (8 other events, 10.0 us)
